TPU v7x, 128 devices: a whole 4x4x4 slice. The times are simulated.
128 devices in a mesh: row: 16 (over x_hi, z, core), col: 8 (over x_lo, y).
Axes of the slice: x: 4 (x_hi: 2, x_lo: 2; x = x_hi * 2 + x_lo), y: 4, z: 4, core: 2. Of those that a mesh axis runs over, the one named last changes fastest.
Arguments:
- tokens: bfloat16 [2048, 6144], P('row', 'col'), may hold values from -6 to 6
- gate_weight: bfloat16 [6144, 8192], P('col', 'row'), may hold values from -0.078125 to 0.078125
- up_weight: bfloat16 [6144, 8192], P('col', 'row'), may hold values from -0.25515518 to 0.25515518
- route: int32 [1024], replicated, may hold values from 0 to 2047
- live: int32 [1024], replicated, may hold values 0 or 1
Outputs:
- panels: float32 [8192, 512], P('col')
- trailing: float32 [8192, 8192], P('col', 'row')
Inputs may be any that keep to these rules, and one draw needn't show every extreme that they name: `route`: indices of tokens routed to the expert; a token may appear more than once.
All inputs are finite; a program needn't handle non-finite values.
Results may differ from a plain program's by a relative error of at most 0.0043.
Values may be sent and summed in bfloat16 or wider, within the bound.
A program may use at most 128 MiB of HBM per device.

v0:
```python
import functools

import jax
import jax.numpy as jnp
from jax import lax
from jax.sharding import Mesh
from jax.sharding import PartitionSpec as P

PANEL = 512
COL = ("col_0", "col_1")
ROW = ("row_0", "row_1", "row_2")
ROW_COL = ("row_0", "row_1", "row_2", "col_0", "col_1")


damping = 0.1


def joined_along(tiles, dim):
    dims = list(tiles.shape[1:])
    dims[dim] *= tiles.shape[0]
    return jnp.moveaxis(tiles, 0, dim).reshape(dims)


def from_everyone(x, axis):
    devices = lax.axis_size(axis)
    return lax.all_to_all(jnp.broadcast_to(x[None], (devices, *x.shape)), axis, 0, 0, tiled=True)


def collect(x, axis, dim):
    return joined_along(from_everyone(x, axis), dim)


def from_root(x, axis, root):
    return lax.dynamic_index_in_dim(lax.all_gather(x, axis), root, 0, keepdims=False)


def by_axis(x, axes):
    return functools.reduce(lax.psum, axes, x)


def rows_for(lines, devices):
    spare = -len(lines) % devices
    return jnp.pad(lines, [(0, spare)] + [(0, 0)] * (lines.ndim - 1))


def broadcast_by_parts(x, axis, root):
    lines = jnp.where(lax.axis_index(axis) == root, x, jnp.zeros_like(x)).reshape(
        -1, *x.shape[1:][-1:]
    )
    padded = rows_for(lines, lax.axis_size(axis))
    own = lax.psum_scatter(padded, axis, scatter_dimension=0, tiled=True)
    return lax.all_gather(own, axis, axis=0, tiled=True)[: len(lines)].reshape(x.shape)


def per_device(tokens, gate_weight, up_weight, route, live):
    col_count = lax.axis_size(COL)
    col_index = lax.axis_index(COL)
    row_index = lax.axis_index(ROW)
    width = gate_weight.shape[1]
    full = width * lax.axis_size(ROW)
    rows_all = route.shape[0]
    own_rows = rows_all // col_count
    tile_rows = full // col_count
    gathered = lax.all_gather(tokens, ROW, axis=0, tiled=True)
    chosen = jnp.take(gathered, route, axis=0)
    joined = jnp.concatenate([gate_weight, up_weight], axis=1)
    sums = lax.psum_scatter(
        jnp.dot(chosen, joined, preferred_element_type=jnp.float32),
        COL,
        scatter_dimension=0,
        tiled=True,
    )
    gate = sums[:, :width]
    up = sums[:, width:]
    mask = lax.dynamic_slice_in_dim(live, col_index * own_rows, own_rows, 0).astype(jnp.float32)
    hidden = (jax.nn.silu(gate) * up * mask[:, None]).astype(jnp.bfloat16)
    stacked = collect(hidden, COL, 0)
    blocks = []
    for half in range(2):
        blocks.append(from_root(stacked, ROW, 2 * col_index + half))
    left = jnp.concatenate(blocks, axis=1)
    gram = lax.dot_general(
        left, stacked, (((0,), (0,)), ((), ())), preferred_element_type=jnp.float32
    )
    down_iota = lax.broadcasted_iota(jnp.int32, (tile_rows, width), 0) + col_index * tile_rows
    across_iota = lax.broadcasted_iota(jnp.int32, (tile_rows, width), 1) + row_index * width
    on_line = down_iota == across_iota
    widened = hidden.astype(jnp.float32)
    term = jnp.sum(widened * widened)
    total = by_axis(term, ROW_COL)
    ridge = damping * total / (rows_all * full)
    matrix = gram / rows_all + jnp.where(on_line, ridge, 0.0)
    corner_block = matrix[0:PANEL, 0:PANEL]
    corner = from_root(corner_block, COL, 0)
    factor = jnp.linalg.cholesky(corner)
    mine = jax.scipy.linalg.solve_triangular(factor, matrix.T, lower=True).T
    panel_down = broadcast_by_parts(mine, ROW, 0)
    offset = row_index % 2 * width
    piece = lax.dynamic_slice_in_dim(panel_down, offset, width, 0)
    panel_across = from_root(piece, COL, row_index // 2)
    matrix = matrix - jnp.dot(
        panel_down,
        panel_across.T,
        precision=lax.Precision.HIGHEST,
        preferred_element_type=jnp.float32,
    )
    return (panel_down, matrix)


def solution(mesh):
    finer = Mesh(mesh.devices.reshape(2, 4, 2, 2, 4), ("row_0", "row_1", "row_2", "col_0", "col_1"))
    placed = (P(ROW, COL), P(COL, ROW), P(COL, ROW), P(), P())
    return jax.shard_map(
        per_device,
        mesh=finer,
        in_specs=placed,
        out_specs=(P(COL, None), P(COL, ROW)),
        check_vma=False,
    )
```

profile of v0, /device:TPU:87, one launch (start us, length us, event | category | flops | bytes accessed | tf_op | source)
XLA Modules:
  0.0 740.6 jit_solution(3962650797941815562)
XLA Ops:
  9.3 50.4 %all-gather.8.cloned.1.call-done = bf16[2048,768]{1,0:T(8,128)(2,1)} async-done(((bf16[128,768]{1,0:T(8,128)(2,1)}), bf16[2048,768]{1,0:T(8,128)(2,1)}) %all-gather.8.cloned.1.call-update) | async-done | bytes 3145744 | tf_op jit(solution)/shard_map/all_gather | solution.py:64
  59.7 6.8 gather_fusion
  72.3 51.5 %reduce-scatter.5.cloned.1.call-done = f32[128,1024]{1,0:T(8,128)} async-done(((f32[1024,1024]{1,0:T(8,128)}), f32[128,1024]{1,0:T(8,128)}) %reduce-scatter.5.cloned.1.call-update) | async-done | bytes 524304 | tf_op jit(solution)/shard_map/reduce_scatter | solution.py:67
  125.6 18.0 %all_to_all.5 = bf16[8,128,512]{2,1,0:T(8,128)(2,1)} all-to-all(bf16[8,128,512]{2,1,0:T(8,128)(2,1)S(1)} %broadcast_in_dim.37), channel_id=1, replica_groups=mesh['row_0'=2,'row_1'=4,'row_2'=2,'col_0'=2,'col_1'=4] {'col_0','col_1'}, dimensions={0} | all-to-all | bytes 2097152 | tf_op jit(solution)/shard_map/all_to_all | solution.py:26
  143.8 5.9 psum.35
  149.7 7.0 psum.36
  156.7 7.2 psum.37
  163.9 5.0 psum.38
  168.9 8.5 %psum.39 = f32[]{:T(128)} all-reduce(f32[]{:T(128)} %psum.38), channel_id=1, replica_groups=mesh['row_0'=2,'row_1'=4,'row_2'=2,'col_0'=2,'col_1'=4] {'col_1'}, use_global_device_ids=true, to_apply=%region_6.7 | all-reduce | flops 1 | bytes 8 | tf_op jit(solution)/shard_map/psum | solution.py:38
  178.1 74.2 %all-gather.10.cloned.1.call-done = bf16[16,1024,512]{2,1,0:T(8,128)(2,1)} async-done(((bf16[1,1024,512]{2,1,0:T(8,128)(2,1)}), bf16[16,1024,512]{2,1,0:T(8,128)(2,1)}) %all-gather.10.cloned.1.call-update) | async-done | bytes 16777232 | tf_op jit(solution)/shard_map/all_gather | solution.py:34
  258.2 89.7 %all-gather.14.cloned.1.call-done = f32[4096,512]{0,1:T(8,128)} async-done(((f32[512,512]{0,1:T(8,128)}), f32[4096,512]{0,1:T(8,128)}) %all-gather.14.cloned.1.call-update) | async-done | bytes 8388624 | tf_op jit(solution)/shard_map/all_gather | solution.py:34
  354.2 11.7 %cholesky.104 = f32[128,128]{1,0:T(8,128)S(1)} custom-call(f32[128,128]{1,0:T(8,128)S(1)} %cholesky.266), custom_call_target="Cholesky" | custom-call | tf_op jit(solution)/shard_map/jit(cholesky)/cholesky | solution.py:95
  366.0 9.8 %custom-call.31 = f32[1,128,128]{1,2,0:T(8,128)S(1)} custom-call(f32[1,128,128]{2,1,0:T(8,128)S(1)} %get-tuple-element.37), custom_call_target="InvertDiagBlocksLowerTriangular" | custom-call | tf_op jit(solution)/shard_map/jit(cholesky)/cholesky | solution.py:95
  378.4 11.7 %cholesky.217 = f32[128,128]{1,0:T(8,128)S(1)} custom-call(f32[128,128]{1,0:T(8,128)S(1)} %cholesky.270), custom_call_target="Cholesky" | custom-call | tf_op jit(solution)/shard_map/jit(cholesky)/cholesky | solution.py:95
  390.1 10.0 %custom-call.32 = f32[1,128,128]{1,2,0:T(8,128)S(1)} custom-call(f32[1,128,128]{2,1,0:T(8,128)S(1)} %get-tuple-element.34), custom_call_target="InvertDiagBlocksLowerTriangular" | custom-call | tf_op jit(solution)/shard_map/jit(cholesky)/cholesky | solution.py:95
  401.7 11.7 %cholesky.238 = f32[128,128]{1,0:T(8,128)S(1)} custom-call(f32[128,128]{1,0:T(8,128)S(1)} %cholesky.275), custom_call_target="Cholesky" | custom-call | tf_op jit(solution)/shard_map/jit(cholesky)/cholesky | solution.py:95
  414.2 9.8 %custom-call.33 = f32[1,128,128]{1,2,0:T(8,128)S(1)} custom-call(f32[1,128,128]{2,1,0:T(8,128)S(1)} %get-tuple-element.31), custom_call_target="InvertDiagBlocksLowerTriangular" | custom-call | tf_op jit(solution)/shard_map/jit(cholesky)/cholesky | solution.py:95
  425.4 11.7 %cholesky.255 = f32[128,128]{1,0:T(8,128)S(1)} custom-call(f32[128,128]{1,0:T(8,128)S(1)} %convolution_subtract_fusion.5), custom_call_target="Cholesky" | custom-call | tf_op jit(solution)/shard_map/jit(cholesky)/cholesky | solution.py:95
  442.4 14.1 %while.1 = (s32[]{:T(128)}, f32[512,512]{1,0:T(8,128)}, s32[4,2]{0,1:T(2,128)S(1)}, f32[4,128,128]{2,1,0:T(8,128)}, s32[]{:T(128)}) while((s32[]{:T(128)}, f32[512,512]{1,0:T(8,128)}, s32[4,2]{0,1:T(2,128)S(1)}, f32[4,128,128]{2,1,0:T(8,128)}, s32[]{:T(128)}) %tuple.36), condition=%wide.while_cond, body=%wide.while_body.sunk | while | flops 2 | bytes 132705 | solution.py:96
  456.5 40.1 %custom-call.34 = f32[4,128,128]{1,2,0:T(8,128)S(1)} custom-call(f32[4,128,128]{2,1,0:T(8,128)} %get-tuple-element.9), custom_call_target="InvertDiagBlocksLowerTriangular" | custom-call | tf_op jit(solution)/shard_map/jit(_solve_triangular)/triangular_solve | solution.py:96
  510.2 68.6 %reduce-scatter.7.cloned.1.call-done = f32[64,512]{1,0:T(8,128)} async-done(((f32[1024,512]{1,0:T(8,128)}), f32[64,512]{1,0:T(8,128)}) %reduce-scatter.7.cloned.1.call-update) | async-done | bytes 131088 | tf_op jit(solution)/shard_map/reduce_scatter | solution.py:51
  579.0 50.1 %all-gather.12.cloned.1.call-done = f32[1024,512]{1,0:T(8,128)} async-done(((f32[64,512]{1,0:T(8,128)}), f32[1024,512]{1,0:T(8,128)}) %all-gather.12.cloned.1.call-update) | async-done | bytes 2097168 | tf_op jit(solution)/shard_map/all_gather | solution.py:52
  631.4 90.9 %all-gather.16.cloned.1.call-done = f32[4096,512]{1,0:T(8,128)} async-done(((f32[512,512]{1,0:T(8,128)}), f32[4096,512]{1,0:T(8,128)}) %all-gather.16.cloned.1.call-update) | async-done | bytes 8388624 | tf_op jit(solution)/shard_map/all_gather | solution.py:34
  722.3 6.7 convolution_subtract_fusion
  (84 shorter events, 65.4 us)
Async XLA Ops:
  7.2 52.5 %all-gather.8.cloned.1.call-start = ((), (), s32[]{:S(2)}) async-start(), calls=%async_computation.3 | async-start | bytes 3342336 | tf_op jit(solution)/shard_map/all_gather | solution.py:64
  7.9 115.9 %reduce-scatter.5.cloned.1.call-start = ((), (), s32[]{:S(2)}) async-start(), calls=%async_computation.4 | async-start | bytes 4718592 | tf_op jit(solution)/shard_map/reduce_scatter | solution.py:67
  9.3 57.2 %copy-start.4 = (bf16[768,512]{1,0:T(8,128)(2,1)S(1)}, bf16[768,512]{1,0:T(8,128)(2,1)}, u32[]{:S(2)}) copy-start(bf16[768,512]{1,0:T(8,128)(2,1)} %param.7) | copy-start | bytes 2359300
  71.4 180.8 %all-gather.10.cloned.1.call-start = ((), (), s32[]{:S(2)}) async-start(), calls=%async_computation.5 | async-start | bytes 17825792 | tf_op jit(solution)/shard_map/all_gather | solution.py:34
  143.7 204.2 %all-gather.14.cloned.1.call-start = ((), (), s32[]{:S(2)}) async-start(), calls=%async_computation.7 | async-start | bytes 9437184 | tf_op jit(solution)/shard_map/all_gather | solution.py:34
  178.1 75.9 %copy-start.1 = (bf16[8,128,512]{2,1,0:T(8,128)(2,1)S(1)}, bf16[8,128,512]{2,1,0:T(8,128)(2,1)}, u32[]{:S(2)}) copy-start(bf16[8,128,512]{2,1,0:T(8,128)(2,1)} %all_to_all.5) | copy-start | bytes 3145732
  258.0 320.9 %reduce-scatter.7.cloned.1.call-start = ((), (), s32[]{:S(2)}) async-start(), calls=%async_computation.9 | async-start | bytes 2228224 | tf_op jit(solution)/shard_map/reduce_scatter | solution.py:51
  353.2 1.0 copy-start.2
  496.6 4.1 copy-start.3
  510.2 118.9 %all-gather.12.cloned.1.call-start = ((), (), s32[]{:S(2)}) async-start(), calls=%async_computation.6 | async-start | bytes 2228224 | tf_op jit(solution)/shard_map/all_gather | solution.py:52
  578.9 143.4 %all-gather.16.cloned.1.call-start = ((), (), s32[]{:S(2)}) async-start(), calls=%async_computation.8 | async-start | bytes 9437184 | tf_op jit(solution)/shard_map/all_gather | solution.py:34
  729.0 3.0 copy-start
Sparse Core Ops, SparseCore 0:
  10.4 49.2 all-gather.7
  71.5 52.1 reduce-scatter.4
  143.8 108.3 all-gather.9
  258.1 89.7 all-gather.13
  510.3 68.5 reduce-scatter.6
  581.2 47.8 all-gather.11
  631.5 90.7 all-gather.15
where the time goes:
time: 750 us; the launch traced here: 741 us
  waiting for transfers between devices  476 us (63%)
  other arithmetic  127 us (17%)
  blocking collectives  51.7 us (7%)
  local copies, waits for them, and re-layouts  38.1 us (5%)
  matrix products  28.7 us (4%)
  between operations  18.1 us (2%)
    all_gather x3, waiting for transfers between devices, from_root(): lax.all_gather(x, axis)  255 us
    another operation x14, other arithmetic, per_device(): factor = jnp.linalg.cholesky(corner)  78.9 us
    reduce_scatter x1, waiting for transfers between devices, broadcast_by_parts(): own = lax.psum_scatter(padded, axis, scatter_dimension=0, tiled=True)  68.6 us
    reduce_scatter x1, waiting for transfers between devices, per_device(): lax.psum_scatter(jnp.dot(chosen, joined, preferred_element_type=jnp.float...  51.5 us
    all_gather x1, waiting for transfers between devices, per_device(): gathered = lax.all_gather(tokens, ROW, axis=0, tiled=True)  50.4 us
    all_gather x1, waiting for transfers between devices, broadcast_by_parts(): lax.all_gather(own, axis, axis=0, tiled=True)[:len(lines)].reshape(x.shape)  50.1 us
    another operation x3, other arithmetic, per_device(): mine = jax.scipy.linalg.solve_triangular(factor, matrix.T, lower=True).T  41.2 us
    psum x5, blocking collectives, by_axis(): return functools.reduce(lax.psum, axes, x)  33.6 us
  transfers between devices with their start and end apart: 7, of which 7 were waited for; matrix products, arithmetic and copies ran while one was open for 0% of the time, Pallas kernels for 0%

commit v1 on v0

--- a/solution.py
+++ b/solution.py
@@ -3,6 +3,8 @@
 import jax
 import jax.numpy as jnp
 from jax import lax
+from jax.experimental import pallas as pl
+from jax.experimental.pallas import tpu as pltpu
 from jax.sharding import Mesh
 from jax.sharding import PartitionSpec as P
 
@@ -10,9 +12,220 @@
 COL = ("col_0", "col_1")
 ROW = ("row_0", "row_1", "row_2")
 ROW_COL = ("row_0", "row_1", "row_2", "col_0", "col_1")
-
+MESH = pl.DeviceIdType.MESH
+F32 = jnp.float32
+BF16 = jnp.bfloat16
 
 damping = 0.1
+
+
+def remote(src, dst, sems, slot, where):
+    send, recv = sems
+    return pltpu.make_async_remote_copy(
+        src_ref=src, dst_ref=dst, send_sem=send.at[slot], recv_sem=recv.at[slot],
+        device_id=where, device_id_type=MESH,
+    )
+
+
+def greet(peers):
+    barrier = pltpu.get_barrier_semaphore()
+    for peer in peers:
+        pl.semaphore_signal(barrier, inc=1, device_id=peer, device_id_type=MESH)
+    pl.semaphore_wait(barrier, len(peers))
+
+
+def hidden_kernel(
+    tok_ref, gate_ref, up_ref, route_ref, live_ref, hidden_ref,
+    tk, gw, uw, tg, tu, rgx, rg1, rg2, ru1, ru2, rux, uout, local_sem,
+    a_send, a_recv, r_send, r_recv,
+):
+    xh, z, core = (lax.axis_index(a) for a in ROW)
+    xl, y = (lax.axis_index(a) for a in COL)
+    oh, oc, ol = 1 - xh, 1 - core, 1 - xl
+    zn, zp, zf = (z + 1) % 4, (z + 3) % 4, (z + 2) % 4
+    yn, yp, yf = (y + 1) % 4, (y + 3) % 4, (y + 2) % 4
+    to_x, to_core = {"row_0": oh}, {"row_2": oc}
+    to_zn, to_zp = {"row_1": zn}, {"row_1": zp}
+    to_l, to_yn, to_yp = {"col_0": ol}, {"col_1": yn}, {"col_1": yp}
+    m = tok_ref.shape[0]
+    half = m // 2
+
+    own = pltpu.make_async_copy(tok_ref, tk.at[xh, z, core], local_sem.at[0])
+    own.start()
+    gcopy = pltpu.make_async_copy(gate_ref, gw, local_sem.at[1])
+    gcopy.start()
+    ucopy = pltpu.make_async_copy(up_ref, uw, local_sem.at[2])
+    ucopy.start()
+    greet([to_x, to_core, to_zn, to_zp, to_l, to_yn, to_yp])
+    own.wait()
+
+    started = []
+    A = (a_send, a_recv)
+
+    def block(h, zz, k, lo=0, n=m):
+        return tk.at[h, zz, k, pl.ds(lo, n)]
+
+    def send(slot, ref, where):
+        copy = remote(ref, ref, A, slot, where)
+        copy.start()
+        started.append(copy)
+
+    def arrive(slot, ref):
+        remote(ref, ref, A, slot, to_x).wait_recv()
+
+    send(0, block(xh, z, core), to_x)
+    send(1, block(xh, z, core), to_zn)
+    send(3, block(xh, z, core), to_zp)
+    send(9, block(xh, z, core), to_core)
+    arrive(1, block(xh, zp, core))
+    send(5, block(xh, zp, core, 0, half), to_zn)
+    arrive(3, block(xh, zn, core))
+    send(7, block(xh, zn, core, half, half), to_zp)
+    send(10, block(xh, zp, core), to_core)
+    send(11, block(xh, zn, core), to_core)
+    arrive(0, block(oh, z, core))
+    send(2, block(oh, z, core), to_zn)
+    send(4, block(oh, z, core), to_zp)
+    send(12, block(oh, z, core), to_core)
+    arrive(5, block(xh, zf, core, 0, half))
+    send(13, block(xh, zf, core, 0, half), to_core)
+    arrive(7, block(xh, zf, core, half, half))
+    send(14, block(xh, zf, core, half, half), to_core)
+    arrive(2, block(oh, zp, core))
+    send(6, block(oh, zp, core, 0, half), to_zn)
+    arrive(4, block(oh, zn, core))
+    send(8, block(oh, zn, core, half, half), to_zp)
+    send(15, block(oh, zp, core), to_core)
+    send(16, block(oh, zn, core), to_core)
+    arrive(6, block(oh, zf, core, 0, half))
+    send(17, block(oh, zf, core, 0, half), to_core)
+    arrive(8, block(oh, zf, core, half, half))
+    send(18, block(oh, zf, core, half, half), to_core)
+    for slot, (h, zz) in ((9, (xh, z)), (10, (xh, zp)), (11, (xh, zn)), (12, (oh, z)),
+                          (15, (oh, zp)), (16, (oh, zn))):
+        arrive(slot, block(h, zz, oc))
+    for slot, h in ((13, xh), (17, oh)):
+        arrive(slot, block(h, zf, oc, 0, half))
+        arrive(slot + 1, block(h, zf, oc, half, half))
+    gcopy.wait()
+    ucopy.wait()
+
+    R = (r_send, r_recv)
+    rows = tg.shape[2]
+    hr = rows // 2
+    pool = 16 * m
+    width = tk.shape[-1]
+
+    def tile(b):
+        spots = jnp.concatenate(
+            [route_ref[pl.ds(pl.multiple_of((e * 4 + b) * rows, rows), rows), :] for e in range(2)], axis=0
+        )
+        hot = (spots == lax.broadcasted_iota(jnp.int32, (2 * rows, pool), 1)).astype(F32).astype(BF16)
+        chosen = jnp.dot(hot, tk[...].reshape(pool, width), preferred_element_type=F32).astype(BF16)
+        g = jnp.dot(chosen, gw[...], preferred_element_type=F32)
+        u = jnp.dot(chosen, uw[...], preferred_element_type=F32)
+        for e in range(2):
+            tg[e, b] = g[e * rows:(e + 1) * rows]
+            tu[e, b] = u[e * rows:(e + 1) * rows]
+
+    def rsend(slot, src, dst, where):
+        copy = remote(src, dst, R, slot, where)
+        copy.start()
+        started.append(copy)
+
+    def rarrive(slot, ref):
+        remote(ref, ref, R, slot, to_l).wait_recv()
+
+    top, bottom = pl.ds(0, hr), pl.ds(hr, hr)
+    tile(yf)
+    rsend(0, tg.at[ol, yf], rgx.at[0], to_l)
+    rsend(4, tu.at[0, yf], ru1.at[0], to_yn)
+    rsend(5, tu.at[1, yf], ru1.at[1], to_yp)
+    tile(yn)
+    rsend(1, tg.at[ol, yn], rgx.at[1], to_l)
+    rsend(6, tu.at[1, yn], ru2.at[0, 1], to_yn)
+    tile(yp)
+    rsend(2, tg.at[ol, yp], rgx.at[2], to_l)
+    rsend(7, tu.at[0, yp], ru2.at[1, 0], to_yp)
+    tile(y)
+    rsend(3, tg.at[ol, y], rgx.at[3], to_l)
+    rarrive(4, ru1.at[0])
+    tu[0, yn] = tu[0, yn] + ru1[0]
+    rsend(8, tu.at[0, yn], ru2.at[0, 0], to_yn)
+    rarrive(5, ru1.at[1])
+    tu[1, yp] = tu[1, yp] + ru1[1]
+    rsend(9, tu.at[1, yp], ru2.at[1, 1], to_yp)
+    rarrive(0, rgx.at[0])
+    tg[xl, yf] = tg[xl, yf] + rgx[0]
+    rsend(10, tg.at[xl, yf, top], rg1.at[0], to_yn)
+    rsend(11, tg.at[xl, yf, bottom], rg1.at[1], to_yp)
+    rarrive(1, rgx.at[1])
+    tg[xl, yn] = tg[xl, yn] + rgx[1]
+    rsend(12, tg.at[xl, yn, bottom], rg2.at[0, bottom], to_yn)
+    rarrive(2, rgx.at[2])
+    tg[xl, yp] = tg[xl, yp] + rgx[2]
+    rsend(13, tg.at[xl, yp, top], rg2.at[1, top], to_yp)
+    rarrive(6, ru2.at[0, 1])
+    rarrive(8, ru2.at[0, 0])
+    rarrive(7, ru2.at[1, 0])
+    rarrive(9, ru2.at[1, 1])
+    uout[...] = tu[ol, y] + ru2[0, ol] + ru2[1, ol]
+    rsend(14, uout, rux, to_l)
+    rarrive(10, rg1.at[0])
+    tg[xl, yn, top] = tg[xl, yn, top] + rg1[0]
+    rsend(15, tg.at[xl, yn, top], rg2.at[0, top], to_yn)
+    rarrive(11, rg1.at[1])
+    tg[xl, yp, bottom] = tg[xl, yp, bottom] + rg1[1]
+    rsend(16, tg.at[xl, yp, bottom], rg2.at[1, bottom], to_yp)
+    rarrive(3, rgx.at[3])
+    rarrive(12, rg2.at[0, bottom])
+    rarrive(13, rg2.at[1, top])
+    rarrive(15, rg2.at[0, top])
+    rarrive(16, rg2.at[1, bottom])
+    rarrive(14, rux)
+    gate = tg[xl, y] + rgx[3] + rg2[0] + rg2[1]
+    up = tu[xl, y] + ru2[0, xl] + ru2[1, xl] + rux[...]
+    mask = live_ref[pl.ds(pl.multiple_of((xl * 4 + y) * rows, rows), rows), :].astype(F32)
+    hidden_ref[...] = (gate / (1.0 + jnp.exp(-gate)) * up * mask).astype(BF16)
+    for copy in started:
+        copy.wait_send()
+
+
+def hidden_of(tokens, gate_weight, up_weight, route, live):
+    m, width = tokens.shape
+    own = gate_weight.shape[1]
+    rows = route.shape[0] // 8
+    hr = rows // 2
+    vm = pltpu.VMEM
+    hbm = pl.BlockSpec(memory_space=pl.ANY)
+    whole = pl.BlockSpec(memory_space=pltpu.VMEM)
+    return pl.pallas_call(
+        hidden_kernel,
+        name="hidden",
+        out_shape=jax.ShapeDtypeStruct((rows, own), BF16),
+        in_specs=[hbm, hbm, hbm, whole, whole],
+        out_specs=whole,
+        scratch_shapes=[
+            vm((2, 4, 2, m, width), BF16),
+            vm(gate_weight.shape, BF16),
+            vm(up_weight.shape, BF16),
+            vm((2, 4, rows, own), F32),
+            vm((2, 4, rows, own), F32),
+            vm((4, rows, own), F32),
+            vm((2, hr, own), F32),
+            vm((2, rows, own), F32),
+            vm((2, rows, own), F32),
+            vm((2, 2, rows, own), F32),
+            vm((rows, own), F32),
+            vm((rows, own), F32),
+            pltpu.SemaphoreType.DMA((3,)),
+            pltpu.SemaphoreType.DMA((19,)),
+            pltpu.SemaphoreType.DMA((19,)),
+            pltpu.SemaphoreType.DMA((17,)),
+            pltpu.SemaphoreType.DMA((17,)),
+        ],
+        compiler_params=pltpu.CompilerParams(collective_id=0, has_side_effects=True, vmem_limit_bytes=60 * 2**20),
+    )(tokens, gate_weight, up_weight, route[:, None], live[:, None])
 
 
 def joined_along(tiles, dim):
@@ -59,21 +272,8 @@
     width = gate_weight.shape[1]
     full = width * lax.axis_size(ROW)
     rows_all = route.shape[0]
-    own_rows = rows_all // col_count
     tile_rows = full // col_count
-    gathered = lax.all_gather(tokens, ROW, axis=0, tiled=True)
-    chosen = jnp.take(gathered, route, axis=0)
-    joined = jnp.concatenate([gate_weight, up_weight], axis=1)
-    sums = lax.psum_scatter(
-        jnp.dot(chosen, joined, preferred_element_type=jnp.float32),
-        COL,
-        scatter_dimension=0,
-        tiled=True,
-    )
-    gate = sums[:, :width]
-    up = sums[:, width:]
-    mask = lax.dynamic_slice_in_dim(live, col_index * own_rows, own_rows, 0).astype(jnp.float32)
-    hidden = (jax.nn.silu(gate) * up * mask[:, None]).astype(jnp.bfloat16)
+    hidden = hidden_of(tokens, gate_weight, up_weight, route, live)
     stacked = collect(hidden, COL, 0)
     blocks = []
     for half in range(2):

time: 750 us -> 693 us (0.924)
  waiting for transfers between devices: 476 us -> 374 us
  Pallas kernels: 0 us -> 54.5 us
    pallas_call x0 -> x1, Pallas kernels: none -> 54.5 us  [hidden_of(): pl.pallas_call(hidden_kernel, name='hidden', out_shape=jax.ShapeDtypeStru...]
    reduce_scatter x1 -> x0, waiting for transfers between devices: 51.5 us -> none  [per_device(): lax.psum_scatter(jnp.dot(chosen, joined, preferred_element_type=jnp.float...]
    all_gather x1 -> x0, waiting for transfers between devices: 50.4 us -> none  [per_device(): gathered = lax.all_gather(tokens, ROW, axis=0, tiled=True)]
  transfers between devices with their start and end apart: 7 -> 5, of which waited for: 7 -> 5; matrix products, arithmetic and copies ran while one was open for 0% -> 0% of each run, Pallas kernels for 0% -> 0%
where the time goes in v1:
time: 693 us; the launch traced here: 681 us
  waiting for transfers between devices  374 us (54%)
  other arithmetic  124 us (18%)
  Pallas kernels  54.5 us (8%)
  blocking collectives  50.8 us (7%)
  local copies, waits for them, and re-layouts  35.8 us (5%)
  matrix products  23.8 us (3%)
  between operations  17.7 us (3%)
    all_gather x3, waiting for transfers between devices, from_root(): lax.all_gather(x, axis)  255 us
    another operation x14, other arithmetic, per_device(): factor = jnp.linalg.cholesky(corner)  78.8 us
    reduce_scatter x1, waiting for transfers between devices, broadcast_by_parts(): own = lax.psum_scatter(padded, axis, scatter_dimension=0, tiled=True)  68.6 us
    pallas_call x1, Pallas kernels, hidden_of(): pl.pallas_call(hidden_kernel, name='hidden', out_shape=jax.ShapeDtypeStru...  54.5 us
    all_gather x1, waiting for transfers between devices, broadcast_by_parts(): lax.all_gather(own, axis, axis=0, tiled=True)[:len(lines)].reshape(x.shape)  50.1 us
    another operation x3, other arithmetic, per_device(): mine = jax.scipy.linalg.solve_triangular(factor, matrix.T, lower=True).T  41.2 us
    psum x5, blocking collectives, by_axis(): return functools.reduce(lax.psum, axes, x)  32 us
    all_to_all x1, blocking collectives, from_everyone(): lax.all_to_all(jnp.broadcast_to(x[None], (devices, *x.shape)), axis, 0, 0...  18.8 us
  transfers between devices with their start and end apart: 5, of which 5 were waited for; matrix products, arithmetic and copies ran while one was open for 0% of the time, Pallas kernels for 0%

profile of v1, /device:TPU:87, one launch (start us, length us, event | category | flops | bytes accessed | tf_op | source)
XLA Modules:
  0.0 680.9 jit_solution(13395144101842253916)
XLA Ops:
  10.6 54.5 %hidden.1 = bf16[128,512]{1,0:T(8,128)(2,1)} custom-call(bf16[128,768]{1,0:T(8,128)(2,1)} %tok_ref.1, bf16[768,512]{1,0:T(8,128)(2,1)} %gate_ref.1, bf16[768,512]{1,0:T(8,128)(2,1)} %up_ref.1, s32[1024,1]{1,0:T(8,128)} %copy.19.route_ref, s32[1024,1]{1,0:T(8,128)} %copy.20.live_ref), custom_call_target="tpu_custom_call" | custom-call | tf_op jit(solution)/shard_map/hidden/pallas_call | solution.py:202
  66.2 18.8 %all_to_all.5 = bf16[8,128,512]{2,1,0:T(8,128)(2,1)} all-to-all(bf16[8,128,512]{2,1,0:T(8,128)(2,1)S(1)} %broadcast_in_dim.29), channel_id=1, replica_groups=mesh['row_0'=2,'row_1'=4,'row_2'=2,'col_0'=2,'col_1'=4] {'col_0','col_1'}, dimensions={0} | all-to-all | bytes 2097152 | tf_op jit(solution)/shard_map/all_to_all | solution.py:239
  85.8 5.9 psum.35
  91.7 6.0 psum.36
  97.7 6.4 psum.37
  104.1 5.0 psum.38
  109.1 8.7 %psum.39 = f32[]{:T(128)} all-reduce(f32[]{:T(128)} %psum.38), channel_id=1, replica_groups=mesh['row_0'=2,'row_1'=4,'row_2'=2,'col_0'=2,'col_1'=4] {'col_1'}, use_global_device_ids=true, to_apply=%region_5.6 | all-reduce | flops 1 | bytes 8 | tf_op jit(solution)/shard_map/psum | solution.py:251
  118.5 74.4 %all-gather.7.cloned.1.call-done = bf16[16,1024,512]{2,1,0:T(8,128)(2,1)} async-done(((bf16[1,1024,512]{2,1,0:T(8,128)(2,1)}), bf16[16,1024,512]{2,1,0:T(8,128)(2,1)}) %all-gather.7.cloned.1.call-update) | async-done | bytes 16777232 | tf_op jit(solution)/shard_map/all_gather | solution.py:247
  198.8 89.7 %all-gather.11.cloned.1.call-done = f32[4096,512]{0,1:T(8,128)} async-done(((f32[512,512]{0,1:T(8,128)}), f32[4096,512]{0,1:T(8,128)}) %all-gather.11.cloned.1.call-update) | async-done | bytes 8388624 | tf_op jit(solution)/shard_map/all_gather | solution.py:247
  294.7 11.7 %cholesky.104 = f32[128,128]{1,0:T(8,128)S(1)} custom-call(f32[128,128]{1,0:T(8,128)S(1)} %cholesky.266), custom_call_target="Cholesky" | custom-call | tf_op jit(solution)/shard_map/jit(cholesky)/cholesky | solution.py:295
  306.6 9.8 %custom-call.31 = f32[1,128,128]{1,2,0:T(8,128)S(1)} custom-call(f32[1,128,128]{2,1,0:T(8,128)S(1)} %get-tuple-element.37), custom_call_target="InvertDiagBlocksLowerTriangular" | custom-call | tf_op jit(solution)/shard_map/jit(cholesky)/cholesky | solution.py:295
  319.0 11.7 %cholesky.217 = f32[128,128]{1,0:T(8,128)S(1)} custom-call(f32[128,128]{1,0:T(8,128)S(1)} %cholesky.270), custom_call_target="Cholesky" | custom-call | tf_op jit(solution)/shard_map/jit(cholesky)/cholesky | solution.py:295
  330.7 10.0 %custom-call.32 = f32[1,128,128]{1,2,0:T(8,128)S(1)} custom-call(f32[1,128,128]{2,1,0:T(8,128)S(1)} %get-tuple-element.34), custom_call_target="InvertDiagBlocksLowerTriangular" | custom-call | tf_op jit(solution)/shard_map/jit(cholesky)/cholesky | solution.py:295
  342.3 11.7 %cholesky.238 = f32[128,128]{1,0:T(8,128)S(1)} custom-call(f32[128,128]{1,0:T(8,128)S(1)} %cholesky.275), custom_call_target="Cholesky" | custom-call | tf_op jit(solution)/shard_map/jit(cholesky)/cholesky | solution.py:295
  354.0 9.8 %custom-call.33 = f32[1,128,128]{1,2,0:T(8,128)S(1)} custom-call(f32[1,128,128]{2,1,0:T(8,128)S(1)} %get-tuple-element.31), custom_call_target="InvertDiagBlocksLowerTriangular" | custom-call | tf_op jit(solution)/shard_map/jit(cholesky)/cholesky | solution.py:295
  365.3 11.7 %cholesky.255 = f32[128,128]{1,0:T(8,128)S(1)} custom-call(f32[128,128]{1,0:T(8,128)S(1)} %convolution_subtract_fusion.5), custom_call_target="Cholesky" | custom-call | tf_op jit(solution)/shard_map/jit(cholesky)/cholesky | solution.py:295
  382.9 14.1 %while.1 = (s32[]{:T(128)}, f32[512,512]{1,0:T(8,128)}, s32[4,2]{0,1:T(2,128)S(1)}, f32[4,128,128]{2,1,0:T(8,128)}, s32[]{:T(128)}) while((s32[]{:T(128)}, f32[512,512]{1,0:T(8,128)}, s32[4,2]{0,1:T(2,128)S(1)}, f32[4,128,128]{2,1,0:T(8,128)}, s32[]{:T(128)}) %tuple.36), condition=%wide.while_cond, body=%wide.while_body.sunk | while | flops 2 | bytes 132205 | solution.py:296
  383.6 2.9 bitcast_dynamic-update-slice_fusion.2
  397.0 40.1 %custom-call.34 = f32[4,128,128]{1,2,0:T(8,128)S(1)} custom-call(f32[4,128,128]{2,1,0:T(8,128)} %get-tuple-element.9), custom_call_target="InvertDiagBlocksLowerTriangular" | custom-call | tf_op jit(solution)/shard_map/jit(_solve_triangular)/triangular_solve | solution.py:296
  450.8 68.6 %reduce-scatter.4.cloned.1.call-done = f32[64,512]{1,0:T(8,128)} async-done(((f32[1024,512]{1,0:T(8,128)}), f32[64,512]{1,0:T(8,128)}) %reduce-scatter.4.cloned.1.call-update) | async-done | bytes 131088 | tf_op jit(solution)/shard_map/reduce_scatter | solution.py:264
  519.5 50.1 %all-gather.9.cloned.1.call-done = f32[1024,512]{1,0:T(8,128)} async-done(((f32[64,512]{1,0:T(8,128)}), f32[1024,512]{1,0:T(8,128)}) %all-gather.9.cloned.1.call-update) | async-done | bytes 2097168 | tf_op jit(solution)/shard_map/all_gather | solution.py:265
  571.9 90.9 %all-gather.13.cloned.1.call-done = f32[4096,512]{1,0:T(8,128)} async-done(((f32[512,512]{1,0:T(8,128)}), f32[4096,512]{1,0:T(8,128)}) %all-gather.13.cloned.1.call-update) | async-done | bytes 8388624 | tf_op jit(solution)/shard_map/all_gather | solution.py:247
  662.9 6.7 convolution_subtract_fusion
  669.5 3.0 copy.25
  (76 shorter events, 54.9 us)
Async XLA Ops:
  7.2 185.6 %all-gather.7.cloned.1.call-start = ((), (), s32[]{:S(2)}) async-start(), calls=%async_computation.2 | async-start | bytes 17825792 | tf_op jit(solution)/shard_map/all_gather | solution.py:247
  65.1 20.0 %copy-start.4 = (bf16[128,512]{1,0:T(8,128)(2,1)S(1)}, bf16[128,512]{1,0:T(8,128)(2,1)}, u32[]{:S(2)}) copy-start(bf16[128,512]{1,0:T(8,128)(2,1)} %hidden.1) | copy-start | bytes 393220
  85.1 203.4 %all-gather.11.cloned.1.call-start = ((), (), s32[]{:S(2)}) async-start(), calls=%async_computation.4 | async-start | bytes 9437184 | tf_op jit(solution)/shard_map/all_gather | solution.py:247
  118.4 76.0 %copy-start.1 = (bf16[8,128,512]{2,1,0:T(8,128)(2,1)S(1)}, bf16[8,128,512]{2,1,0:T(8,128)(2,1)}, u32[]{:S(2)}) copy-start(bf16[8,128,512]{2,1,0:T(8,128)(2,1)} %all_to_all.5) | copy-start | bytes 3145732
  198.6 320.9 %reduce-scatter.4.cloned.1.call-start = ((), (), s32[]{:S(2)}) async-start(), calls=%async_computation.6 | async-start | bytes 2228224 | tf_op jit(solution)/shard_map/reduce_scatter | solution.py:264
  293.7 1.0 copy-start.2
  437.2 4.1 copy-start.3
  450.7 118.9 %all-gather.9.cloned.1.call-start = ((), (), s32[]{:S(2)}) async-start(), calls=%async_computation.3 | async-start | bytes 2228224 | tf_op jit(solution)/shard_map/all_gather | solution.py:265
  519.4 143.4 %all-gather.13.cloned.1.call-start = ((), (), s32[]{:S(2)}) async-start(), calls=%async_computation.5 | async-start | bytes 9437184 | tf_op jit(solution)/shard_map/all_gather | solution.py:247
  669.5 3.0 copy-start
Sparse Core Ops, SparseCore 0:
  85.2 107.5 all-gather.6
  198.7 89.7 all-gather.10
  450.8 68.5 reduce-scatter.3
  521.7 47.8 all-gather.8
  572.0 90.7 all-gather.12

commit v2 on v1

--- a/solution.py
+++ b/solution.py
@@ -228,83 +228,383 @@
     )(tokens, gate_weight, up_weight, route[:, None], live[:, None])
 
 
-def joined_along(tiles, dim):
-    dims = list(tiles.shape[1:])
-    dims[dim] *= tiles.shape[0]
-    return jnp.moveaxis(tiles, 0, dim).reshape(dims)
-
-
-def from_everyone(x, axis):
-    devices = lax.axis_size(axis)
-    return lax.all_to_all(jnp.broadcast_to(x[None], (devices, *x.shape)), axis, 0, 0, tiled=True)
-
-
-def collect(x, axis, dim):
-    return joined_along(from_everyone(x, axis), dim)
-
-
-def from_root(x, axis, root):
-    return lax.dynamic_index_in_dim(lax.all_gather(x, axis), root, 0, keepdims=False)
-
-
-def by_axis(x, axes):
-    return functools.reduce(lax.psum, axes, x)
-
-
-def rows_for(lines, devices):
-    spare = -len(lines) % devices
-    return jnp.pad(lines, [(0, spare)] + [(0, 0)] * (lines.ndim - 1))
-
-
-def broadcast_by_parts(x, axis, root):
-    lines = jnp.where(lax.axis_index(axis) == root, x, jnp.zeros_like(x)).reshape(
-        -1, *x.shape[1:][-1:]
-    )
-    padded = rows_for(lines, lax.axis_size(axis))
-    own = lax.psum_scatter(padded, axis, scatter_dimension=0, tiled=True)
-    return lax.all_gather(own, axis, axis=0, tiled=True)[: len(lines)].reshape(x.shape)
+NB = 128
+HIGH = lax.Precision.HIGHEST
+
+
+def spread(x):
+    return jnp.broadcast_to(x, (8, NB))
+
+
+def tile_inverse(rows):
+    count = len(rows)
+    lane = lax.broadcasted_iota(jnp.int32, (8, NB), 1)
+    sub = lax.broadcasted_iota(jnp.int32, (8, NB), 0)
+    rows = list(rows)
+    out = []
+    for g in range(count):
+        column = [[spread(rows[i][:, 8 * g + c:8 * g + c + 1]) for c in range(8)] for i in range(g, count)]
+        e = [[spread(column[0][b][a:a + 1, :]) for b in range(a + 1)] for a in range(8)]
+        inside = (lane >= 8 * g) & (lane < 8 * g + 8)
+        rows[g] = jnp.where(inside, (lane == sub + 8 * g).astype(F32), rows[g])
+        for i in range(g + 1, count):
+            rows[i] = jnp.where(inside, 0.0, rows[i])
+        pivots = e[0][0]
+        for c in range(8):
+            if c:
+                pivots = jnp.where(sub == c, e[c][c], pivots)
+            inverse = 1.0 / e[c][c]
+            for a in range(c + 1, 8):
+                factor = e[a][c] * inverse
+                for b in range(c + 1, a + 1):
+                    e[a][b] = e[a][b] - factor * e[b][c]
+            pivot_row = spread(rows[g][c:c + 1, :])
+            for i in range(g, count):
+                factor = column[i - g][c] * inverse
+                if i == g:
+                    factor = jnp.where(sub > c, factor, 0.0)
+                for b in range(c + 1, 8):
+                    column[i - g][b] = column[i - g][b] - factor * e[b][c]
+                rows[i] = rows[i] - factor * pivot_row
+        out.append(jnp.where(lane <= sub + 8 * g, rows[g] * lax.rsqrt(pivots), 0.0))
+    return out
+
+
+def dot_t(a, b):
+    return lax.dot_general(a, b, (((1,), (1,)), ((), ())), precision=HIGH, preferred_element_type=F32)
+
+
+def dot(a, b):
+    return jnp.dot(a, b, precision=HIGH, preferred_element_type=F32)
+
+
+def factor_inverse(a_ref, x_ref, between):
+    n = a_ref.shape[0]
+    x_ref[...] = jnp.zeros_like(x_ref)
+    for k in range(n // NB):
+        lo, hi = k * NB, (k + 1) * NB
+        part = tile_inverse([a_ref[lo + 8 * i:lo + 8 * i + 8, lo:hi] for i in range(NB // 8)])
+        for i, rows in enumerate(part):
+            x_ref[lo + 8 * i:lo + 8 * i + 8, lo:hi] = rows
+        x = x_ref[lo:hi, lo:hi]
+        if hi < n:
+            low = dot_t(a_ref[hi:, lo:hi], x)
+            a_ref[hi:, lo:hi] = low
+            a_ref[hi:, hi:] = a_ref[hi:, hi:] - dot_t(low, low)
+        between(k)
+        if k:
+            x_ref[lo:hi, :lo] = -dot(x, dot(a_ref[lo:hi, :lo], x_ref[:lo, :lo]))
+
+
+def cross(a, b):
+    return lax.dot_general(a, b, (((0,), (0,)), ((), ())), preferred_element_type=F32)
+
+
+def factor_kernel(
+    total_rows, full, hid_ref, hp_ref, hcol_ref, hl_ref, x_ref, ridge_ref,
+    corner, tr, tc, own_sem, p1s, p1r, p2s, p2r, p3s, p3r, ts, tr_sem, us, ur, hs, hr_sem, qs, qr, ls, lr,
+):
+    xh, z, core = (lax.axis_index(a) for a in ROW)
+    xl, y = (lax.axis_index(a) for a in COL)
+    oh, oc = 1 - xh, 1 - core
+    zn, zp, zf = (z + 1) % 4, (z + 3) % 4, (z + 2) % 4
+    ci, ki = xl * 4 + y, xh * 4 + z
+    ri = ki * 2 + core
+    to_x, to_core = {"row_0": oh}, {"row_2": oc}
+    to_zn, to_zp = {"row_1": zn}, {"row_1": zp}
+    mirror = {"row_0": xl, "row_1": y, "col_0": xh, "col_1": z}
+    away = jnp.logical_or(xh != xl, z != y)
+    rows = hid_ref.shape[0]
+    half = rows // 2
+    col_steps = [(a, b) for a in range(2) for b in range(4) if a + b]
+    row_steps = [(a, b, c) for a in range(2) for b in range(4) for c in range(2) if a + b + c]
+    col_peer = {s: {"col_0": (xl + s[0]) % 2, "col_1": (y + s[1]) % 4} for s in col_steps}
+    col_from = {s: (xl + s[0]) % 2 * 4 + (y + 4 - s[1]) % 4 for s in col_steps}
+    row_peer = {s: {"row_0": (xh + s[0]) % 2, "row_1": (z + s[1]) % 4, "row_2": (core + s[2]) % 2} for s in row_steps}
+    row_from = {s: ((xh + s[0]) % 2 * 4 + (z + 4 - s[1]) % 4) * 2 + (core + s[2]) % 2 for s in row_steps}
+
+    barrier = pltpu.get_barrier_semaphore()
+    for peer in list(col_peer.values()) + list(row_peer.values()):
+        pl.semaphore_signal(barrier, inc=1, device_id=peer, device_id_type=MESH)
+
+    @pl.when(away)
+    def _():
+        pl.semaphore_signal(barrier, inc=1, device_id=mirror, device_id_type=MESH)
+
+    hcopy = pltpu.make_async_copy(hid_ref, hcol_ref.at[ci], own_sem.at[0])
+    hcopy.start()
+    squares = jnp.zeros((8, 128), F32)
+    for i in range(0, rows, 8):
+        for j in range(0, hid_ref.shape[1], 128):
+            part = hid_ref[pl.ds(i, 8), pl.ds(j, 128)].astype(F32)
+            squares = squares + part * part
+    tr[ri] = squares
+    peers = len(col_steps) + len(row_steps)
+
+    @pl.when(away)
+    def _():
+        pl.semaphore_wait(barrier, peers + 1)
+
+    @pl.when(jnp.logical_not(away))
+    def _():
+        pl.semaphore_wait(barrier, peers)
+
+    started = []
+
+    def send(sems, slot, src, dst, where):
+        copy = remote(src, dst, sems, slot, where)
+        copy.start()
+        started.append(copy)
+
+    def arrive(sems, slot, ref):
+        remote(ref, ref, sems, slot, to_core).wait_recv()
+
+    mine = hp_ref.at[ci, pl.ds(pl.multiple_of(core * half, half), half)]
+    at_root = jnp.logical_and(xh == 0, z == 0)
+    holder = jnp.logical_and(at_root, core == 0)
+    one = (p1s, p1r)
+    give = remote(hid_ref.at[pl.ds(half, half)], hp_ref.at[ci, pl.ds(half, half)], (p1s, p1r), 0, to_core)
+    keep = pltpu.make_async_copy(hid_ref.at[pl.ds(0, half)], hp_ref.at[ci, pl.ds(0, half)], own_sem.at[1])
+    hop_x = pltpu.make_async_remote_copy(mine, mine, p1s.at[1], p1r.at[0], device_id=to_x, device_id_type=MESH)
+    hop_n = pltpu.make_async_remote_copy(mine, mine, p1s.at[2], p1r.at[0], device_id=to_zn, device_id_type=MESH)
+    hop_p = pltpu.make_async_remote_copy(mine, mine, p1s.at[3], p1r.at[0], device_id=to_zp, device_id_type=MESH)
+
+    @pl.when(holder)
+    def _():
+        give.start()
+        keep.start()
+        keep.wait()
+
+    @pl.when(jnp.logical_not(holder))
+    def _():
+        arrive(one, 0, mine)
+
+    @pl.when(at_root)
+    def _():
+        hop_x.start()
+
+    @pl.when(z <= 1)
+    def _():
+        hop_n.start()
+
+    @pl.when(z == 0)
+    def _():
+        hop_p.start()
+
+    two, three = (p2s, p2r), (p3s, p3r)
+    for s in col_steps:
+        send(two, s[0] * 4 + s[1], mine, mine, col_peer[s])
+    send(three, 0, mine, mine, to_core)
+    for s in row_steps:
+        send((ts, tr_sem), s[0] * 8 + s[1] * 2 + s[2], tr.at[ri], tr.at[ri], row_peer[s])
+
+    across = remote(hid_ref, hl_ref.at[core, ci], (qs, qr), 0, mirror)
+    stay = pltpu.make_async_copy(hid_ref, hl_ref.at[core, ci], own_sem.at[2])
+
+    @pl.when(away)
+    def _():
+        across.start()
+
+    @pl.when(jnp.logical_not(away))
+    def _():
+        stay.start()
+
+    for s in row_steps:
+        arrive((ts, tr_sem), s[0] * 8 + s[1] * 2 + s[2], tr.at[row_from[s]])
+    tc[ci] = jnp.sum(tr[...], axis=0)
+    order = [(0, 1), (0, 3), (1, 0), (0, 2), (1, 1), (1, 3), (1, 2)]
+    for s in order[:3]:
+        slot = s[0] * 4 + s[1]
+        ref = hp_ref.at[col_from[s], pl.ds(pl.multiple_of(core * half, half), half)]
+        arrive(two, slot, ref)
+        send(three, slot, ref, ref, to_core)
+    for s in col_steps:
+        send((us, ur), s[0] * 4 + s[1], tc.at[ci], tc.at[ci], col_peer[s])
+    for s in order[3:]:
+        slot = s[0] * 4 + s[1]
+        ref = hp_ref.at[col_from[s], pl.ds(pl.multiple_of(core * half, half), half)]
+        arrive(two, slot, ref)
+        send(three, slot, ref, ref, to_core)
+
+    four, five, six = (hs, hr_sem), (qs, qr), (ls, lr)
+
+    def block(h, zz, k, lo=0, n=rows):
+        return hl_ref.at[k, h * 4 + zz, pl.ds(lo, n)]
+
+    def pass_on(sems, slot, ref, where):
+        send(sems, slot, ref, ref, where)
+
+    @pl.when(away)
+    def _():
+        across.wait_recv()
+
+    @pl.when(jnp.logical_not(away))
+    def _():
+        stay.wait()
+
+    pass_on(five, 1, block(xh, z, core), to_x)
+    pass_on(five, 2, block(xh, z, core), to_zn)
+    pass_on(five, 3, block(xh, z, core), to_zp)
+    for s in order:
+        send(four, s[0] * 4 + s[1], hid_ref, hcol_ref.at[ci], col_peer[s])
+
+    arrive(three, 0, hp_ref.at[ci, pl.ds(pl.multiple_of(oc * half, half), half)])
+    for s in order:
+        arrive(three, s[0] * 4 + s[1], hp_ref.at[col_from[s], pl.ds(pl.multiple_of(oc * half, half), half)])
+    for s in col_steps:
+        arrive((us, ur), s[0] * 4 + s[1], tc.at[col_from[s]])
+    total = jnp.sum(jnp.sum(tc[...], axis=0), axis=(0, 1), keepdims=True)
+    ridge = damping * total / (total_rows * full)
+    ridge_ref[...] = jnp.broadcast_to(ridge, (8, 128))
+    panel = corner.shape[0]
+    hp = hp_ref[...].reshape(total_rows, panel)
+    on_line = lax.broadcasted_iota(jnp.int32, (panel, panel), 0) == lax.broadcasted_iota(jnp.int32, (panel, panel), 1)
+    corner[...] = cross(hp, hp) / total_rows + jnp.where(on_line, ridge, 0.0)
+
+    def between(k):
+        if k == 0:
+            pass_on(six, 0, block(xh, z, core), to_core)
+            arrive(five, 2, block(xh, zp, core))
+            pass_on(five, 4, block(xh, zp, core, 0, half), to_zn)
+            pass_on(six, 1, block(xh, zp, core), to_core)
+            arrive(five, 3, block(xh, zn, core))
+            pass_on(five, 5, block(xh, zn, core, half, half), to_zp)
+            pass_on(six, 2, block(xh, zn, core), to_core)
+            arrive(five, 1, block(oh, z, core))
+            pass_on(five, 6, block(oh, z, core), to_zn)
+            pass_on(five, 7, block(oh, z, core), to_zp)
+            pass_on(six, 3, block(oh, z, core), to_core)
+        elif k == 1:
+            arrive(five, 6, block(oh, zp, core))
+            pass_on(five, 8, block(oh, zp, core, 0, half), to_zn)
+            pass_on(six, 4, block(oh, zp, core), to_core)
+            arrive(five, 7, block(oh, zn, core))
+            pass_on(five, 9, block(oh, zn, core, half, half), to_zp)
+            pass_on(six, 5, block(oh, zn, core), to_core)
+        elif k == 2:
+            arrive(five, 4, block(xh, zf, core, 0, half))
+            arrive(five, 5, block(xh, zf, core, half, half))
+            pass_on(six, 6, block(xh, zf, core), to_core)
+            arrive(five, 8, block(oh, zf, core, 0, half))
+            arrive(five, 9, block(oh, zf, core, half, half))
+            pass_on(six, 7, block(oh, zf, core), to_core)
+
+    factor_inverse(corner, x_ref, between)
+    for slot, (h, zz) in enumerate(((xh, z), (xh, zp), (xh, zn), (oh, z), (oh, zp), (oh, zn), (xh, zf), (oh, zf))):
+        arrive(six, slot, block(h, zz, oc))
+    for s in order:
+        arrive(four, s[0] * 4 + s[1], hcol_ref.at[col_from[s]])
+    hcopy.wait()
+    for copy in started:
+        copy.wait_send()
+
+    @pl.when(away)
+    def _():
+        across.wait_send()
+
+    @pl.when(holder)
+    def _():
+        give.wait_send()
+
+    @pl.when(at_root)
+    def _():
+        hop_x.wait_send()
+
+    @pl.when(z <= 1)
+    def _():
+        hop_n.wait_send()
+
+    @pl.when(z == 0)
+    def _():
+        hop_p.wait_send()
+
+
+def factor_of(hidden, rows_all, full):
+    rows, own = hidden.shape
+    whole = pl.BlockSpec(memory_space=pltpu.VMEM)
+    dma = pltpu.SemaphoreType.DMA
+    return pl.pallas_call(
+        functools.partial(factor_kernel, rows_all, full),
+        name="factor",
+        out_shape=(
+            jax.ShapeDtypeStruct((8, rows, own), BF16),
+            jax.ShapeDtypeStruct((8, rows, own), BF16),
+            jax.ShapeDtypeStruct((2, 8, rows, own), BF16),
+            jax.ShapeDtypeStruct((PANEL, PANEL), F32),
+            jax.ShapeDtypeStruct((8, 128), F32),
+        ),
+        in_specs=[whole],
+        out_specs=(whole,) * 5,
+        scratch_shapes=[
+            pltpu.VMEM((PANEL, PANEL), F32),
+            pltpu.VMEM((16, 8, 128), F32),
+            pltpu.VMEM((8, 8, 128), F32),
+            dma((3,)),
+            dma((4,)), dma((1,)),
+            dma((8,)), dma((8,)),
+            dma((8,)), dma((8,)),
+            dma((16,)), dma((16,)),
+            dma((8,)), dma((8,)),
+            dma((8,)), dma((8,)),
+            dma((10,)), dma((10,)),
+            dma((8,)), dma((8,)),
+        ],
+        compiler_params=pltpu.CompilerParams(collective_id=1, has_side_effects=True, vmem_limit_bytes=60 * 2**20),
+    )(hidden)
+
+
+def pair(a):
+    high = a.astype(BF16)
+    return high, (a - high.astype(F32)).astype(BF16)
+
+
+def dot3_t(a, b):
+    def one(u, v):
+        return lax.dot_general(u, v, (((1,), (1,)), ((), ())), preferred_element_type=F32)
+
+    return one(a[0], b[0]) + (one(a[0], b[1]) + one(a[1], b[0]))
+
+
+def outputs_kernel(hp_ref, hcol_ref, hl_ref, x_ref, ridge_ref, panel_ref, trailing_ref):
+    xh, z, core = (lax.axis_index(a) for a in ROW)
+    xl, y = (lax.axis_index(a) for a in COL)
+    ci, ri = xl * 4 + y, (xh * 4 + z) * 2 + core
+    rows_all = hp_ref.shape[0] * hp_ref.shape[1]
+    n = x_ref.shape[0]
+    ridge = ridge_ref[0:1, 0:1]
+    on_line = lax.broadcasted_iota(jnp.int32, (n, n), 0) == lax.broadcasted_iota(jnp.int32, (n, n), 1)
+    hp = hp_ref[...].reshape(rows_all, n)
+    hcol = hcol_ref[...].reshape(rows_all, n)
+    x = pair(x_ref[...])
+
+    def with_ridge(gram, here):
+        return gram / rows_all + jnp.where(jnp.logical_and(on_line, here), ridge, 0.0)
+
+    right = pair(dot3_t(pair(with_ridge(cross(hcol, hp), ri == 0)), x))
+    for j in range(2):
+        left = hl_ref[j].reshape(rows_all, n)
+        down = dot3_t(pair(with_ridge(cross(left, hp), ci * 2 + j == 0)), x)
+        panel_ref[pl.ds(j * n, n), :] = down
+        trailing_ref[pl.ds(j * n, n), :] = with_ridge(cross(left, hcol), ci * 2 + j == ri) - dot3_t(pair(down), right)
+
+
+def outputs_of(hp, hcol, hl, x, ridge):
+    n = x.shape[0]
+    whole = pl.BlockSpec(memory_space=pltpu.VMEM)
+    return pl.pallas_call(
+        outputs_kernel,
+        name="outputs",
+        out_shape=(jax.ShapeDtypeStruct((2 * n, n), F32), jax.ShapeDtypeStruct((2 * n, n), F32)),
+        in_specs=[whole] * 5,
+        out_specs=(whole, whole),
+        compiler_params=pltpu.CompilerParams(vmem_limit_bytes=60 * 2**20),
+    )(hp, hcol, hl, x, ridge)
 
 
 def per_device(tokens, gate_weight, up_weight, route, live):
-    col_count = lax.axis_size(COL)
-    col_index = lax.axis_index(COL)
-    row_index = lax.axis_index(ROW)
-    width = gate_weight.shape[1]
-    full = width * lax.axis_size(ROW)
-    rows_all = route.shape[0]
-    tile_rows = full // col_count
+    full = gate_weight.shape[1] * lax.axis_size(ROW)
     hidden = hidden_of(tokens, gate_weight, up_weight, route, live)
-    stacked = collect(hidden, COL, 0)
-    blocks = []
-    for half in range(2):
-        blocks.append(from_root(stacked, ROW, 2 * col_index + half))
-    left = jnp.concatenate(blocks, axis=1)
-    gram = lax.dot_general(
-        left, stacked, (((0,), (0,)), ((), ())), preferred_element_type=jnp.float32
-    )
-    down_iota = lax.broadcasted_iota(jnp.int32, (tile_rows, width), 0) + col_index * tile_rows
-    across_iota = lax.broadcasted_iota(jnp.int32, (tile_rows, width), 1) + row_index * width
-    on_line = down_iota == across_iota
-    widened = hidden.astype(jnp.float32)
-    term = jnp.sum(widened * widened)
-    total = by_axis(term, ROW_COL)
-    ridge = damping * total / (rows_all * full)
-    matrix = gram / rows_all + jnp.where(on_line, ridge, 0.0)
-    corner_block = matrix[0:PANEL, 0:PANEL]
-    corner = from_root(corner_block, COL, 0)
-    factor = jnp.linalg.cholesky(corner)
-    mine = jax.scipy.linalg.solve_triangular(factor, matrix.T, lower=True).T
-    panel_down = broadcast_by_parts(mine, ROW, 0)
-    offset = row_index % 2 * width
-    piece = lax.dynamic_slice_in_dim(panel_down, offset, width, 0)
-    panel_across = from_root(piece, COL, row_index // 2)
-    matrix = matrix - jnp.dot(
-        panel_down,
-        panel_across.T,
-        precision=lax.Precision.HIGHEST,
-        preferred_element_type=jnp.float32,
-    )
-    return (panel_down, matrix)
+    return outputs_of(*factor_of(hidden, route.shape[0], full))
 
 
 def solution(mesh):

time: 693 us -> 132 us (0.19)
  the two profiles are of different devices: /device:TPU:87 before, /device:TPU:1 now
where the time goes in v2:
time: 132 us
  Pallas kernels  128 us (97%)
  local copies, waits for them, and re-layouts  3.41 us (3%)
    pallas_call x1, Pallas kernels, hidden_of(): pl.pallas_call(hidden_kernel, name='hidden', out_shape=jax.ShapeDtypeStru...  58.9 us
    pallas_call x1, Pallas kernels, factor_of(): pl.pallas_call(functools.partial(factor_kernel, rows_all, full), name='fa...  58.4 us
    pallas_call x1, Pallas kernels, outputs_of(): pl.pallas_call(outputs_kernel, name='outputs', out_shape=(jax.ShapeDtypeS...  10.9 us

profile of v2, /device:TPU:1, one launch (start us, length us, event | category | flops | bytes accessed | tf_op | source)
XLA Modules:
  0.0 132.3 jit_solution(12749558829307572472)
XLA Ops:
  0.6 1.7 %copy.7.route_ref = s32[1024,1]{1,0:T(8,128)} copy(s32[1024,1]{0,1:T(1,128)} %bitcast.2) | data formatting | bytes 8192 | tf_op jit(solution)/shard_map/broadcast_in_dim | solution.py:228
  2.3 1.7 %copy.8.live_ref = s32[1024,1]{1,0:T(8,128)} copy(s32[1024,1]{0,1:T(1,128)} %bitcast.3) | data formatting | bytes 8192 | tf_op jit(solution)/shard_map/broadcast_in_dim | solution.py:228
  4.0 58.9 %hidden.1.hid_ref = bf16[128,512]{1,0:T(8,128)(2,1)} custom-call(bf16[128,768]{1,0:T(8,128)(2,1)} %tok_ref.1, bf16[768,512]{1,0:T(8,128)(2,1)} %gate_ref.1, bf16[768,512]{1,0:T(8,128)(2,1)} %up_ref.1, s32[1024,1]{1,0:T(8,128)} %copy.7.route_ref, s32[1024,1]{1,0:T(8,128)} %copy.8.live_ref), custom_call_target="tpu_custom_call" | custom-call | tf_op jit(solution)/shard_map/hidden/pallas_call | solution.py:202
  63.0 58.4 %factor.1 = (bf16[8,128,512]{2,1,0:T(8,128)(2,1)}, bf16[8,128,512]{2,1,0:T(8,128)(2,1)}, bf16[2,8,128,512]{3,2,1,0:T(8,128)(2,1)}, f32[512,512]{1,0:T(8,128)}, f32[8,128]{1,0:T(8,128)}) custom-call(bf16[128,512]{1,0:T(8,128)(2,1)} %hidden.1.hid_ref), custom_call_target="tpu_custom_call" | custom-call | tf_op jit(solution)/shard_map/factor/pallas_call | solution.py:526
  121.4 10.9 %outputs.1 = (f32[1024,512]{1,0:T(8,128)}, f32[1024,512]{1,0:T(8,128)}) custom-call(bf16[8,128,512]{2,1,0:T(8,128)(2,1)} %get-tuple-element.7.hp_ref, bf16[8,128,512]{2,1,0:T(8,128)(2,1)} %get-tuple-element.8.hcol_ref, bf16[2,8,128,512]{3,2,1,0:T(8,128)(2,1)} %get-tuple-element.9.hl_ref, f32[512,512]{1,0:T(8,128)} %get-tuple-element.10.x_ref, ...), custom_call_target="tpu_custom_call" | custom-call | tf_op jit(solution)/shard_map/outputs/pallas_call | solution.py:594

commit v3 on v0

v3 whole, which is shorter than its diff:
```python
import functools

import jax
import jax.numpy as jnp
from jax import lax
from jax.experimental import pallas as pl
from jax.experimental.pallas import tpu as pltpu
from jax.sharding import Mesh
from jax.sharding import PartitionSpec as P

PANEL = 512
COL = ("col_0", "col_1")
ROW = ("row_0", "row_1", "row_2")
ROW_COL = ("row_0", "row_1", "row_2", "col_0", "col_1")
MESH = pl.DeviceIdType.MESH
F32 = jnp.float32
BF16 = jnp.bfloat16

damping = 0.1


def remote(src, dst, sems, slot, where):
    send, recv = sems
    return pltpu.make_async_remote_copy(
        src_ref=src, dst_ref=dst, send_sem=send.at[slot], recv_sem=recv.at[slot],
        device_id=where, device_id_type=MESH,
    )


NB = 128
HIGH = lax.Precision.HIGHEST


def spread(x):
    return jnp.broadcast_to(x, (8, NB))


def tile_inverse(rows):
    count = len(rows)
    lane = lax.broadcasted_iota(jnp.int32, (8, NB), 1)
    sub = lax.broadcasted_iota(jnp.int32, (8, NB), 0)
    rows = list(rows)
    out = []
    for g in range(count):
        column = [[spread(rows[i][:, 8 * g + c:8 * g + c + 1]) for c in range(8)] for i in range(g, count)]
        e = [[spread(column[0][b][a:a + 1, :]) for b in range(a + 1)] for a in range(8)]
        inside = (lane >= 8 * g) & (lane < 8 * g + 8)
        rows[g] = jnp.where(inside, (lane == sub + 8 * g).astype(F32), rows[g])
        for i in range(g + 1, count):
            rows[i] = jnp.where(inside, 0.0, rows[i])
        pivots = e[0][0]
        for c in range(8):
            if c:
                pivots = jnp.where(sub == c, e[c][c], pivots)
            inverse = 1.0 / e[c][c]
            for a in range(c + 1, 8):
                factor = e[a][c] * inverse
                for b in range(c + 1, a + 1):
                    e[a][b] = e[a][b] - factor * e[b][c]
            pivot_row = spread(rows[g][c:c + 1, :])
            for i in range(g, count):
                factor = column[i - g][c] * inverse
                if i == g:
                    factor = jnp.where(sub > c, factor, 0.0)
                for b in range(c + 1, 8):
                    column[i - g][b] = column[i - g][b] - factor * e[b][c]
                rows[i] = rows[i] - factor * pivot_row
        out.append(jnp.where(lane <= sub + 8 * g, rows[g] * lax.rsqrt(pivots), 0.0))
    return out


def dot_t(a, b):
    return lax.dot_general(a, b, (((1,), (1,)), ((), ())), precision=HIGH, preferred_element_type=F32)


def dot(a, b):
    return jnp.dot(a, b, precision=HIGH, preferred_element_type=F32)


def factor_inverse(a_ref, x_ref, between):
    n = a_ref.shape[0]
    x_ref[...] = jnp.zeros_like(x_ref)
    for k in range(n // NB):
        lo, hi = k * NB, (k + 1) * NB
        part = tile_inverse([a_ref[lo + 8 * i:lo + 8 * i + 8, lo:hi] for i in range(NB // 8)])
        for i, rows in enumerate(part):
            x_ref[lo + 8 * i:lo + 8 * i + 8, lo:hi] = rows
        x = x_ref[lo:hi, lo:hi]
        if hi < n:
            low = dot_t(a_ref[hi:, lo:hi], x)
            a_ref[hi:, lo:hi] = low
            a_ref[hi:, hi:] = a_ref[hi:, hi:] - dot_t(low, low)
        between(k)
        if k:
            x_ref[lo:hi, :lo] = -dot(x, dot(a_ref[lo:hi, :lo], x_ref[:lo, :lo]))


def cross(a, b):
    return lax.dot_general(a, b, (((0,), (0,)), ((), ())), preferred_element_type=F32)


def turned(row):
    return jnp.broadcast_to(row, (128, 128)).astype(F32).T


def main_kernel(
    total_rows, full, tok_ref, gate_ref, up_ref, route_ref, live_ref,
    hp_ref, hcol_ref, hl_ref, x_ref, ridge_ref,
    tk, gw, uw, spots, tg, tu, rgx, rg1, rg2, ru1, ru2, rux, uout, hid, corner, tr, tc, own_sem,
    a_send, a_recv, r_send, r_recv, p1s, p1r, p2s, p2r, p3s, p3r, ts, tq, us, ur, hs, hr_sem, qs, qr, ls, lr,
):
    xh, z, core = (lax.axis_index(a) for a in ROW)
    xl, y = (lax.axis_index(a) for a in COL)
    oh, oc, ol = 1 - xh, 1 - core, 1 - xl
    zn, zp, zf = (z + 1) % 4, (z + 3) % 4, (z + 2) % 4
    yn, yp, yf = (y + 1) % 4, (y + 3) % 4, (y + 2) % 4
    ci, ki = xl * 4 + y, xh * 4 + z
    ri = ki * 2 + core
    to_x, to_core = {"row_0": oh}, {"row_2": oc}
    to_zn, to_zp, to_zf = {"row_1": zn}, {"row_1": zp}, {"row_1": zf}
    to_l, to_yn, to_yp = {"col_0": ol}, {"col_1": yn}, {"col_1": yp}
    mirror = {"row_0": xl, "row_1": y, "col_0": xh, "col_1": z}
    away = jnp.logical_or(xh != xl, z != y)
    m = tok_ref.shape[0]
    cut = m * 5 // 8
    col_steps = [(a, b) for a in range(2) for b in range(4) if a + b]
    row_steps = [(a, b, c) for a in range(2) for b in range(4) for c in range(2) if a + b + c]
    col_peer = {s: {"col_0": (xl + s[0]) % 2, "col_1": (y + s[1]) % 4} for s in col_steps}
    col_from = {s: (xl + s[0]) % 2 * 4 + (y + 4 - s[1]) % 4 for s in col_steps}
    row_peer = {s: {"row_0": (xh + s[0]) % 2, "row_1": (z + s[1]) % 4, "row_2": (core + s[2]) % 2} for s in row_steps}
    row_from = {s: ((xh + s[0]) % 2 * 4 + (z + 4 - s[1]) % 4) * 2 + (core + s[2]) % 2 for s in row_steps}

    own = pltpu.make_async_copy(tok_ref, tk.at[xh, z, core], own_sem.at[0])
    own.start()
    gcopy = pltpu.make_async_copy(gate_ref, gw, own_sem.at[1])
    gcopy.start()
    ucopy = pltpu.make_async_copy(up_ref, uw, own_sem.at[2])
    ucopy.start()
    barrier = pltpu.get_barrier_semaphore()
    for peer in list(col_peer.values()) + list(row_peer.values()):
        pl.semaphore_signal(barrier, inc=1, device_id=peer, device_id_type=MESH)

    @pl.when(away)
    def _():
        pl.semaphore_signal(barrier, inc=1, device_id=mirror, device_id_type=MESH)

    rows = total_rows // 8
    for t in range(8):
        spots[pl.ds(t * rows, rows), :] = turned(route_ref[t:t + 1, :]).astype(jnp.int32)
    own.wait()
    peers = len(col_steps) + len(row_steps)

    @pl.when(away)
    def _():
        pl.semaphore_wait(barrier, peers + 1)

    @pl.when(jnp.logical_not(away))
    def _():
        pl.semaphore_wait(barrier, peers)

    started = []

    def send(sems, slot, src, dst, where):
        copy = remote(src, dst, sems, slot, where)
        copy.start()
        started.append(copy)

    def arrive(sems, slot, ref):
        remote(ref, ref, sems, slot, to_core).wait_recv()

    def pass_on(sems, slot, ref, where):
        send(sems, slot, ref, ref, where)

    A = (a_send, a_recv)

    def block(h, zz, k, lo=0, n=m):
        return tk.at[h, zz, k, pl.ds(lo, n)]

    pass_on(A, 0, block(xh, z, core), to_x)
    pass_on(A, 1, block(xh, z, core), to_zn)
    pass_on(A, 2, block(xh, z, core), to_zp)
    pass_on(A, 3, block(xh, z, core), to_zf)
    pass_on(A, 10, block(xh, z, core), to_core)
    arrive(A, 1, block(xh, zp, core))
    pass_on(A, 7, block(xh, zp, core, cut, m - cut), to_x)
    pass_on(A, 11, block(xh, zp, core), to_core)
    arrive(A, 2, block(xh, zn, core))
    pass_on(A, 8, block(xh, zn, core, cut, m - cut), to_x)
    pass_on(A, 12, block(xh, zn, core), to_core)
    arrive(A, 0, block(oh, z, core))
    pass_on(A, 4, block(oh, z, core, 0, cut), to_zn)
    pass_on(A, 5, block(oh, z, core, 0, cut), to_zp)
    pass_on(A, 6, block(oh, z, core, 0, cut), to_zf)
    pass_on(A, 14, block(oh, z, core), to_core)
    arrive(A, 3, block(xh, zf, core))
    pass_on(A, 9, block(xh, zf, core, cut, m - cut), to_x)
    pass_on(A, 13, block(xh, zf, core), to_core)
    for slot, zz in ((0, zp), (1, zn), (2, zf)):
        arrive(A, 4 + slot, block(oh, zz, core, 0, cut))
        arrive(A, 7 + slot, block(oh, zz, core, cut, m - cut))
        pass_on(A, 15 + slot, block(oh, zz, core), to_core)
    for slot, (h, zz) in enumerate(((xh, z), (xh, zp), (xh, zn), (xh, zf), (oh, z), (oh, zp), (oh, zn), (oh, zf))):
        arrive(A, 10 + slot, block(h, zz, oc))
    gcopy.wait()
    ucopy.wait()

    R = (r_send, r_recv)
    hr = rows // 2
    pool = 16 * m
    width = tk.shape[-1]

    def tile(b):
        spot = jnp.concatenate(
            [spots[pl.ds(pl.multiple_of((e * 4 + b) * rows, rows), rows), :] for e in range(2)], axis=0
        )
        spot = jnp.concatenate([spot] * (pool // 128), axis=1)
        hot = (spot == lax.broadcasted_iota(jnp.int32, (2 * rows, pool), 1)).astype(F32).astype(BF16)
        chosen = jnp.dot(hot, tk[...].reshape(pool, width), preferred_element_type=F32).astype(BF16)
        g = jnp.dot(chosen, gw[...], preferred_element_type=F32)
        u = jnp.dot(chosen, uw[...], preferred_element_type=F32)
        for e in range(2):
            tg[e, b] = g[e * rows:(e + 1) * rows]
            tu[e, b] = u[e * rows:(e + 1) * rows]

    top, bottom = pl.ds(0, hr), pl.ds(hr, hr)
    tile(yf)
    send(R, 0, tg.at[ol, yf], rgx.at[0], to_l)
    send(R, 4, tu.at[0, yf], ru1.at[0], to_yn)
    send(R, 5, tu.at[1, yf], ru1.at[1], to_yp)
    tile(yn)
    send(R, 1, tg.at[ol, yn], rgx.at[1], to_l)
    send(R, 6, tu.at[1, yn], ru2.at[0, 1], to_yn)
    tile(yp)
    send(R, 2, tg.at[ol, yp], rgx.at[2], to_l)
    send(R, 7, tu.at[0, yp], ru2.at[1, 0], to_yp)
    tile(y)
    send(R, 3, tg.at[ol, y], rgx.at[3], to_l)
    arrive(R, 4, ru1.at[0])
    tu[0, yn] = tu[0, yn] + ru1[0]
    send(R, 8, tu.at[0, yn], ru2.at[0, 0], to_yn)
    arrive(R, 5, ru1.at[1])
    tu[1, yp] = tu[1, yp] + ru1[1]
    send(R, 9, tu.at[1, yp], ru2.at[1, 1], to_yp)
    arrive(R, 0, rgx.at[0])
    tg[xl, yf] = tg[xl, yf] + rgx[0]
    send(R, 10, tg.at[xl, yf, top], rg1.at[0], to_yn)
    send(R, 11, tg.at[xl, yf, bottom], rg1.at[1], to_yp)
    arrive(R, 1, rgx.at[1])
    tg[xl, yn] = tg[xl, yn] + rgx[1]
    send(R, 12, tg.at[xl, yn, bottom], rg2.at[0, bottom], to_yn)
    arrive(R, 2, rgx.at[2])
    tg[xl, yp] = tg[xl, yp] + rgx[2]
    send(R, 13, tg.at[xl, yp, top], rg2.at[1, top], to_yp)
    arrive(R, 6, ru2.at[0, 1])
    arrive(R, 8, ru2.at[0, 0])
    arrive(R, 7, ru2.at[1, 0])
    arrive(R, 9, ru2.at[1, 1])
    uout[...] = tu[ol, y] + ru2[0, ol] + ru2[1, ol]
    send(R, 14, uout, rux, to_l)
    arrive(R, 10, rg1.at[0])
    tg[xl, yn, top] = tg[xl, yn, top] + rg1[0]
    send(R, 15, tg.at[xl, yn, top], rg2.at[0, top], to_yn)
    arrive(R, 11, rg1.at[1])
    tg[xl, yp, bottom] = tg[xl, yp, bottom] + rg1[1]
    send(R, 16, tg.at[xl, yp, bottom], rg2.at[1, bottom], to_yp)
    mask = jnp.concatenate([turned(live_ref[pl.ds(ci, 1), :])] * (hid.shape[1] // 128), axis=1)
    arrive(R, 3, rgx.at[3])
    arrive(R, 12, rg2.at[0, bottom])
    arrive(R, 13, rg2.at[1, top])
    arrive(R, 15, rg2.at[0, top])
    arrive(R, 16, rg2.at[1, bottom])
    gate = tg[xl, y] + rgx[3] + rg2[0] + rg2[1]
    part = tu[xl, y] + ru2[0, xl] + ru2[1, xl]
    act = gate / (1.0 + jnp.exp(-gate)) * mask
    arrive(R, 14, rux)
    made = (act * (part + rux[...])).astype(BF16)
    hid[...] = made
    hcol_ref[ci] = made

    half = rows // 2
    at_root = jnp.logical_and(xh == 0, z == 0)
    holder = jnp.logical_and(at_root, core == 0)

    def by_half(c, k):
        return hp_ref.at[c, pl.ds(pl.multiple_of(k * half, half), half)]

    mine = by_half(ci, core)
    give = remote(hid.at[pl.ds(half, half)], hp_ref.at[ci, pl.ds(half, half)], (p1s, p1r), 0, to_core)
    hops = [
        pltpu.make_async_remote_copy(mine, mine, p1s.at[1 + i], p1r.at[0], device_id=where, device_id_type=MESH)
        for i, where in enumerate((to_x, to_zn, to_zp, to_zf))
    ]

    @pl.when(holder)
    def _():
        hp_ref[ci, pl.ds(0, half)] = made[:half]
        give.start()

    wide = made.astype(F32)
    squares = jnp.zeros((8, 128), F32)
    for i in range(0, rows, 8):
        for j in range(0, hid.shape[1], 128):
            piece = wide[i:i + 8, j:j + 128]
            squares = squares + piece * piece
    tr[ri] = squares
    for s in row_steps:
        send((ts, tq), s[0] * 8 + s[1] * 2 + s[2], tr.at[ri], tr.at[ri], row_peer[s])

    @pl.when(jnp.logical_not(holder))
    def _():
        arrive((p1s, p1r), 0, mine)

    @pl.when(at_root)
    def _():
        hops[0].start()

    @pl.when(z == 0)
    def _():
        for hop in hops[1:]:
            hop.start()

    two, three = (p2s, p2r), (p3s, p3r)
    order = [(1, 2), (1, 1), (1, 3), (0, 2), (0, 1), (0, 3), (1, 0)]
    for s in order:
        send(two, s[0] * 4 + s[1], mine, mine, col_peer[s])
    pass_on(three, 0, mine, to_core)
    across = remote(hid, hl_ref.at[core, ci], (qs, qr), 0, mirror)
    stay = pltpu.make_async_copy(hid, hl_ref.at[core, ci], own_sem.at[0])

    @pl.when(away)
    def _():
        across.start()

    @pl.when(jnp.logical_not(away))
    def _():
        stay.start()

    four, five, six = (hs, hr_sem), (qs, qr), (ls, lr)
    for s in order:
        send(four, s[0] * 4 + s[1], hid, hcol_ref.at[ci], col_peer[s])
    for s in row_steps:
        arrive((ts, tq), s[0] * 8 + s[1] * 2 + s[2], tr.at[row_from[s]])
    tc[ci] = jnp.sum(tr[...], axis=0)
    for s in col_steps:
        send((us, ur), s[0] * 4 + s[1], tc.at[ci], tc.at[ci], col_peer[s])
    for s in order[::-1]:
        slot = s[0] * 4 + s[1]
        arrive(two, slot, by_half(col_from[s], core))
        pass_on(three, slot, by_half(col_from[s], core), to_core)

    def spread_block(h, zz, k):
        return hl_ref.at[k, h * 4 + zz]

    here = spread_block(xh, z, core)

    @pl.when(away)
    def _():
        across.wait_recv()

    @pl.when(jnp.logical_not(away))
    def _():
        stay.wait()

    for slot, where in ((1, to_x), (2, to_zn), (3, to_zp), (4, to_zf)):
        pass_on(five, slot, here, where)
    arrive(three, 0, by_half(ci, oc))
    for s in order[::-1]:
        arrive(three, s[0] * 4 + s[1], by_half(col_from[s], oc))
    panel = corner.shape[0]
    hp = hp_ref[...].reshape(total_rows, panel)
    on_line = lax.broadcasted_iota(jnp.int32, (panel, panel), 0) == lax.broadcasted_iota(jnp.int32, (panel, panel), 1)
    gram = cross(hp, hp) / total_rows
    for s in col_steps:
        arrive((us, ur), s[0] * 4 + s[1], tc.at[col_from[s]])
    total = jnp.sum(jnp.sum(tc[...], axis=0), axis=(0, 1), keepdims=True)
    ridge = damping * total / (total_rows * full)
    ridge_ref[...] = jnp.broadcast_to(ridge, (8, 128))
    corner[...] = gram + jnp.where(on_line, ridge, 0.0)

    def between(k):
        if k == 0:
            pass_on(six, 0, here, to_core)
            arrive(five, 1, spread_block(oh, z, core))
            for slot, where in ((5, to_zn), (6, to_zp), (7, to_zf)):
                pass_on(five, slot, spread_block(oh, z, core), where)
            pass_on(six, 1, spread_block(oh, z, core), to_core)
        elif k == 1:
            for slot, zz in ((2, zp), (3, zn), (4, zf)):
                arrive(five, slot, spread_block(xh, zz, core))
                pass_on(six, slot, spread_block(xh, zz, core), to_core)
        elif k == 2:
            for slot, zz in ((5, zp), (6, zn), (7, zf)):
                arrive(five, slot, spread_block(oh, zz, core))
                pass_on(six, slot, spread_block(oh, zz, core), to_core)

    factor_inverse(corner, x_ref, between)
    for slot, (h, zz) in enumerate(((xh, z), (oh, z), (xh, zp), (xh, zn), (xh, zf), (oh, zp), (oh, zn), (oh, zf))):
        arrive(six, slot, spread_block(h, zz, oc))
    for s in order:
        arrive(four, s[0] * 4 + s[1], hcol_ref.at[col_from[s]])
    for copy in started:
        copy.wait_send()

    @pl.when(away)
    def _():
        across.wait_send()

    @pl.when(holder)
    def _():
        give.wait_send()

    @pl.when(at_root)
    def _():
        hops[0].wait_send()

    @pl.when(z == 0)
    def _():
        for hop in hops[1:]:
            hop.wait_send()


def main_of(tokens, gate_weight, up_weight, route, live, full):
    m, width = tokens.shape
    own = gate_weight.shape[1]
    rows_all = route.shape[0]
    rows = rows_all // 8
    hr = rows // 2
    vm = pltpu.VMEM
    dma = pltpu.SemaphoreType.DMA
    hbm = pl.BlockSpec(memory_space=pl.ANY)
    whole = pl.BlockSpec(memory_space=pltpu.VMEM)
    return pl.pallas_call(
        functools.partial(main_kernel, rows_all, full),
        name="hidden_factor",
        out_shape=(
            jax.ShapeDtypeStruct((8, rows, own), BF16),
            jax.ShapeDtypeStruct((8, rows, own), BF16),
            jax.ShapeDtypeStruct((2, 8, rows, own), BF16),
            jax.ShapeDtypeStruct((PANEL, PANEL), F32),
            jax.ShapeDtypeStruct((8, 128), F32),
        ),
        in_specs=[hbm, hbm, hbm, whole, whole],
        out_specs=(whole,) * 5,
        scratch_shapes=[
            vm((2, 4, 2, m, width), BF16),
            vm(gate_weight.shape, BF16),
            vm(up_weight.shape, BF16),
            vm((rows_all, 128), jnp.int32),
            vm((2, 4, rows, own), F32),
            vm((2, 4, rows, own), F32),
            vm((4, rows, own), F32),
            vm((2, hr, own), F32),
            vm((2, rows, own), F32),
            vm((2, rows, own), F32),
            vm((2, 2, rows, own), F32),
            vm((rows, own), F32),
            vm((rows, own), F32),
            vm((rows, own), BF16),
            vm((PANEL, PANEL), F32),
            vm((16, 8, 128), F32),
            vm((8, 8, 128), F32),
            dma((3,)),
            dma((18,)), dma((18,)),
            dma((17,)), dma((17,)),
            dma((5,)), dma((1,)),
            dma((8,)), dma((8,)),
            dma((8,)), dma((8,)),
            dma((16,)), dma((16,)),
            dma((8,)), dma((8,)),
            dma((8,)), dma((8,)),
            dma((8,)), dma((8,)),
            dma((8,)), dma((8,)),
        ],
        compiler_params=pltpu.CompilerParams(collective_id=0, has_side_effects=True, vmem_limit_bytes=60 * 2**20),
    )(tokens, gate_weight, up_weight, route.reshape(8, rows), live.reshape(8, rows))


def pair(a):
    high = a.astype(BF16)
    return high, (a - high.astype(F32)).astype(BF16)


def dot3_t(a, b):
    def one(u, v):
        return lax.dot_general(u, v, (((1,), (1,)), ((), ())), preferred_element_type=F32)

    return one(a[0], b[0]) + (one(a[0], b[1]) + one(a[1], b[0]))


def outputs_kernel(hp_ref, hcol_ref, hl_ref, x_ref, ridge_ref, panel_ref, trailing_ref):
    xh, z, core = (lax.axis_index(a) for a in ROW)
    xl, y = (lax.axis_index(a) for a in COL)
    ci, ri = xl * 4 + y, (xh * 4 + z) * 2 + core
    rows_all = hp_ref.shape[0] * hp_ref.shape[1]
    n = x_ref.shape[0]
    ridge = ridge_ref[0:1, 0:1]
    on_line = lax.broadcasted_iota(jnp.int32, (n, n), 0) == lax.broadcasted_iota(jnp.int32, (n, n), 1)
    hp = hp_ref[...].reshape(rows_all, n)
    hcol = hcol_ref[...].reshape(rows_all, n)
    x = pair(x_ref[...])

    def with_ridge(gram, here):
        return gram / rows_all + jnp.where(jnp.logical_and(on_line, here), ridge, 0.0)

    right = pair(dot3_t(pair(with_ridge(cross(hcol, hp), ri == 0)), x))
    for j in range(2):
        left = hl_ref[j].reshape(rows_all, n)
        down = dot3_t(pair(with_ridge(cross(left, hp), ci * 2 + j == 0)), x)
        panel_ref[pl.ds(j * n, n), :] = down
        trailing_ref[pl.ds(j * n, n), :] = with_ridge(cross(left, hcol), ci * 2 + j == ri) - dot3_t(pair(down), right)


def outputs_of(hp, hcol, hl, x, ridge):
    n = x.shape[0]
    whole = pl.BlockSpec(memory_space=pltpu.VMEM)
    return pl.pallas_call(
        outputs_kernel,
        name="outputs",
        out_shape=(jax.ShapeDtypeStruct((2 * n, n), F32), jax.ShapeDtypeStruct((2 * n, n), F32)),
        in_specs=[whole] * 5,
        out_specs=(whole, whole),
        compiler_params=pltpu.CompilerParams(vmem_limit_bytes=60 * 2**20),
    )(hp, hcol, hl, x, ridge)


def per_device(tokens, gate_weight, up_weight, route, live):
    full = gate_weight.shape[1] * lax.axis_size(ROW)
    return outputs_of(*main_of(tokens, gate_weight, up_weight, route, live, full))


def solution(mesh):
    finer = Mesh(mesh.devices.reshape(2, 4, 2, 2, 4), ("row_0", "row_1", "row_2", "col_0", "col_1"))
    placed = (P(ROW, COL), P(COL, ROW), P(COL, ROW), P(), P())
    return jax.shard_map(
        per_device,
        mesh=finer,
        in_specs=placed,
        out_specs=(P(COL, None), P(COL, ROW)),
        check_vma=False,
    )
```

time: 750 us -> 126 us (0.17); the launches traced: 741 us -> 125 us
  waiting for transfers between devices: 476 us -> 0 us
  other arithmetic: 127 us -> 0 us
  Pallas kernels: 0 us -> 124 us
  blocking collectives: 51.7 us -> 0 us
  local copies, waits for them, and re-layouts: 38.1 us -> 0 us
  matrix products: 28.7 us -> 0 us
  between operations: 18.1 us -> 0.64 us
    all_gather x5 -> x0, waiting for transfers between devices: 355 us -> none  [the longest x3 255 us: from_root(): lax.all_gather(x, axis)]
    pallas_call x0 -> x2, Pallas kernels: none -> 124 us  [the longest x1 113 us: main_of(): pl.pallas_call(functools.partial(main_kernel, rows_all, full), name='hidd...]
    reduce_scatter x2 -> x0, waiting for transfers between devices: 120 us -> none  [the longest x1 68.6 us: broadcast_by_parts(): own = lax.psum_scatter(padded, axis, scatter_dimension=0, tiled=True)]
    another operation x17 -> x0, other arithmetic: 120 us -> none  [the longest x14 78.9 us: per_device(): factor = jnp.linalg.cholesky(corner)]
    psum x5 -> x0, blocking collectives: 33.6 us -> none  [by_axis(): return functools.reduce(lax.psum, axes, x)]
    all_to_all x1 -> x0, blocking collectives: 18 us -> none  [from_everyone(): lax.all_to_all(jnp.broadcast_to(x[None], (devices, *x.shape)), axis, 0, 0...]
    another operation x13 -> x0, matrix products: 14.5 us -> none  [the longest x7 9.03 us: per_device(): mine = jax.scipy.linalg.solve_triangular(factor, matrix.T, lower=True).T]
    another operation x17 -> x0, local copies, waits for them, and re-layouts: 14.3 us -> none
  transfers between devices with their start and end apart: 7 -> 0, of which waited for: 7 -> 0; matrix products, arithmetic and copies ran while one was open for 0% -> 0% of each run, Pallas kernels for 0% -> 0%
where the time goes in v3:
time: 126 us; the launch traced here: 125 us
  Pallas kernels  124 us (98%)
    pallas_call x1, Pallas kernels, main_of(): pl.pallas_call(functools.partial(main_kernel, rows_all, full), name='hidd...  113 us
    pallas_call x1, Pallas kernels, outputs_of(): pl.pallas_call(outputs_kernel, name='outputs', out_shape=(jax.ShapeDtypeS...  10.9 us

profile of v3, /device:TPU:87, one launch (start us, length us, event | category | flops | bytes accessed | tf_op | source)
XLA Modules:
  0.0 124.6 jit_solution(138099850140331154)
XLA Ops:
  0.6 113.0 %hidden_factor.1 = (bf16[8,128,512]{2,1,0:T(8,128)(2,1)}, bf16[8,128,512]{2,1,0:T(8,128)(2,1)}, bf16[2,8,128,512]{3,2,1,0:T(8,128)(2,1)}, f32[512,512]{1,0:T(8,128)}, f32[8,128]{1,0:T(8,128)}) custom-call(bf16[128,768]{1,0:T(8,128)(2,1)} %tok_ref.1, bf16[768,512]{1,0:T(8,128)(2,1)} %gate_ref.1, bf16[768,512]{1,0:T(8,128)(2,1)} %up_ref.1, s32[8,128]{1,0:T(8,128)} %bitcast.2, ...), custom_call_target="tpu_custom_call" | custom-call | tf_op jit(solution)/shard_map/hidden_factor/pallas_call | solution.py:432
  113.7 10.9 %outputs.1 = (f32[1024,512]{1,0:T(8,128)}, f32[1024,512]{1,0:T(8,128)}) custom-call(bf16[8,128,512]{2,1,0:T(8,128)(2,1)} %get-tuple-element.7.hp_ref, bf16[8,128,512]{2,1,0:T(8,128)(2,1)} %get-tuple-element.8.hcol_ref, bf16[2,8,128,512]{3,2,1,0:T(8,128)(2,1)} %get-tuple-element.9.hl_ref, f32[512,512]{1,0:T(8,128)} %get-tuple-element.10.x_ref, ...), custom_call_target="tpu_custom_call" | custom-call | tf_op jit(solution)/shard_map/outputs/pallas_call | solution.py:516

commit v4 on v3

--- a/solution.py
+++ b/solution.py
@@ -35,7 +35,7 @@
     return jnp.broadcast_to(x, (8, NB))
 
 
-def tile_inverse(rows):
+def tile_inverse(rows, halfway):
     count = len(rows)
     lane = lax.broadcasted_iota(jnp.int32, (8, NB), 1)
     sub = lax.broadcasted_iota(jnp.int32, (8, NB), 0)
@@ -52,7 +52,11 @@
         for c in range(8):
             if c:
                 pivots = jnp.where(sub == c, e[c][c], pivots)
-            inverse = 1.0 / e[c][c]
+            if c % 2 == 0:
+                inverse = 1.0 / e[c][c]
+                later = e[c][c] / (e[c][c] * e[c + 1][c + 1] - e[c + 1][c] * e[c + 1][c])
+            else:
+                inverse = later
             for a in range(c + 1, 8):
                 factor = e[a][c] * inverse
                 for b in range(c + 1, a + 1):
@@ -66,6 +70,8 @@
                     column[i - g][b] = column[i - g][b] - factor * e[b][c]
                 rows[i] = rows[i] - factor * pivot_row
         out.append(jnp.where(lane <= sub + 8 * g, rows[g] * lax.rsqrt(pivots), 0.0))
+        if g == count // 2 - 1:
+            halfway()
     return out
 
 
@@ -82,7 +88,9 @@
     x_ref[...] = jnp.zeros_like(x_ref)
     for k in range(n // NB):
         lo, hi = k * NB, (k + 1) * NB
-        part = tile_inverse([a_ref[lo + 8 * i:lo + 8 * i + 8, lo:hi] for i in range(NB // 8)])
+        part = tile_inverse(
+            [a_ref[lo + 8 * i:lo + 8 * i + 8, lo:hi] for i in range(NB // 8)], lambda: between(2 * k)
+        )
         for i, rows in enumerate(part):
             x_ref[lo + 8 * i:lo + 8 * i + 8, lo:hi] = rows
         x = x_ref[lo:hi, lo:hi]
@@ -90,7 +98,7 @@
             low = dot_t(a_ref[hi:, lo:hi], x)
             a_ref[hi:, lo:hi] = low
             a_ref[hi:, hi:] = a_ref[hi:, hi:] - dot_t(low, low)
-        between(k)
+        between(2 * k + 1)
         if k:
             x_ref[lo:hi, :lo] = -dot(x, dot(a_ref[lo:hi, :lo], x_ref[:lo, :lo]))
 
@@ -197,10 +205,14 @@
     pass_on(A, 13, block(xh, zf, core), to_core)
     for slot, zz in ((0, zp), (1, zn), (2, zf)):
         arrive(A, 4 + slot, block(oh, zz, core, 0, cut))
+        pass_on(A, 15 + slot, block(oh, zz, core, 0, cut), to_core)
         arrive(A, 7 + slot, block(oh, zz, core, cut, m - cut))
-        pass_on(A, 15 + slot, block(oh, zz, core), to_core)
-    for slot, (h, zz) in enumerate(((xh, z), (xh, zp), (xh, zn), (xh, zf), (oh, z), (oh, zp), (oh, zn), (oh, zf))):
+        pass_on(A, 18 + slot, block(oh, zz, core, cut, m - cut), to_core)
+    for slot, (h, zz) in enumerate(((xh, z), (xh, zp), (xh, zn), (xh, zf), (oh, z))):
         arrive(A, 10 + slot, block(h, zz, oc))
+    for slot, zz in ((0, zp), (1, zn), (2, zf)):
+        arrive(A, 15 + slot, block(oh, zz, oc, 0, cut))
+        arrive(A, 18 + slot, block(oh, zz, oc, cut, m - cut))
     gcopy.wait()
     ucopy.wait()
 
@@ -320,12 +332,20 @@
             hop.start()
 
     two, three = (p2s, p2r), (p3s, p3r)
-    order = [(1, 2), (1, 1), (1, 3), (0, 2), (0, 1), (0, 3), (1, 0)]
-    for s in order:
-        send(two, s[0] * 4 + s[1], mine, mine, col_peer[s])
-    pass_on(three, 0, mine, to_core)
+    along = ((1, to_yn), (3, to_yp), (2, {"col_1": yf}))
     across = remote(hid, hl_ref.at[core, ci], (qs, qr), 0, mirror)
     stay = pltpu.make_async_copy(hid, hl_ref.at[core, ci], own_sem.at[0])
+    four, five, six = (hs, hr_sem), (qs, qr), (ls, lr)
+    cp = ol * 4 + y
+    pass_on(two, 4, mine, to_l)
+    for d, where in along:
+        pass_on(two, d, mine, where)
+    pass_on(three, 0, mine, to_core)
+    arrive(two, 4, by_half(cp, core))
+    for d, where in along:
+        pass_on(two, 4 + d, by_half(cp, core), where)
+    pass_on(three, 4, by_half(cp, core), to_core)
+    send(four, 4, hid, hcol_ref.at[ci], to_l)
 
     @pl.when(away)
     def _():
@@ -335,15 +355,15 @@
     def _():
         stay.start()
 
-    four, five, six = (hs, hr_sem), (qs, qr), (ls, lr)
-    for s in order:
-        send(four, s[0] * 4 + s[1], hid, hcol_ref.at[ci], col_peer[s])
     for s in row_steps:
         arrive((ts, tq), s[0] * 8 + s[1] * 2 + s[2], tr.at[row_from[s]])
     tc[ci] = jnp.sum(tr[...], axis=0)
     for s in col_steps:
         send((us, ur), s[0] * 4 + s[1], tc.at[ci], tc.at[ci], col_peer[s])
-    for s in order[::-1]:
+    for d, where in along:
+        send(four, d, hid, hcol_ref.at[ci], where)
+    order = [(0, 1), (0, 3), (0, 2), (1, 1), (1, 3), (1, 2)]
+    for s in order:
         slot = s[0] * 4 + s[1]
         arrive(two, slot, by_half(col_from[s], core))
         pass_on(three, slot, by_half(col_from[s], core), to_core)
@@ -352,19 +372,9 @@
         return hl_ref.at[k, h * 4 + zz]
 
     here = spread_block(xh, z, core)
-
-    @pl.when(away)
-    def _():
-        across.wait_recv()
-
-    @pl.when(jnp.logical_not(away))
-    def _():
-        stay.wait()
-
-    for slot, where in ((1, to_x), (2, to_zn), (3, to_zp), (4, to_zf)):
-        pass_on(five, slot, here, where)
     arrive(three, 0, by_half(ci, oc))
-    for s in order[::-1]:
+    arrive(three, 4, by_half(cp, oc))
+    for s in order:
         arrive(three, s[0] * 4 + s[1], by_half(col_from[s], oc))
     panel = corner.shape[0]
     hp = hp_ref[...].reshape(total_rows, panel)
@@ -375,25 +385,42 @@
     total = jnp.sum(jnp.sum(tc[...], axis=0), axis=(0, 1), keepdims=True)
     ridge = damping * total / (total_rows * full)
     ridge_ref[...] = jnp.broadcast_to(ridge, (8, 128))
-    corner[...] = gram + jnp.where(on_line, ridge, 0.0)
+    scale = 1.0 / ridge
+    corner[...] = (gram + jnp.where(on_line, ridge, 0.0)) * scale
 
     def between(k):
         if k == 0:
+            arrive(four, 4, hcol_ref.at[cp])
+            for d, where in along:
+                pass_on(four, 4 + d, hcol_ref.at[cp], where)
+
+            @pl.when(away)
+            def _():
+                across.wait_recv()
+
+            @pl.when(jnp.logical_not(away))
+            def _():
+                stay.wait()
+
+            for slot, where in ((1, to_x), (2, to_zn), (3, to_zp), (4, to_zf)):
+                pass_on(five, slot, here, where)
             pass_on(six, 0, here, to_core)
+        elif k == 3:
             arrive(five, 1, spread_block(oh, z, core))
             for slot, where in ((5, to_zn), (6, to_zp), (7, to_zf)):
                 pass_on(five, slot, spread_block(oh, z, core), where)
             pass_on(six, 1, spread_block(oh, z, core), to_core)
-        elif k == 1:
+        elif k == 4:
             for slot, zz in ((2, zp), (3, zn), (4, zf)):
                 arrive(five, slot, spread_block(xh, zz, core))
                 pass_on(six, slot, spread_block(xh, zz, core), to_core)
-        elif k == 2:
+        elif k == 6:
             for slot, zz in ((5, zp), (6, zn), (7, zf)):
                 arrive(five, slot, spread_block(oh, zz, core))
                 pass_on(six, slot, spread_block(oh, zz, core), to_core)
 
     factor_inverse(corner, x_ref, between)
+    x_ref[...] = x_ref[...] * jnp.sqrt(scale)
     for slot, (h, zz) in enumerate(((xh, z), (oh, z), (xh, zp), (xh, zn), (xh, zf), (oh, zp), (oh, zn), (oh, zf))):
         arrive(six, slot, spread_block(h, zz, oc))
     for s in order:
@@ -427,7 +454,7 @@
     hr = rows // 2
     vm = pltpu.VMEM
     dma = pltpu.SemaphoreType.DMA
-    hbm = pl.BlockSpec(memory_space=pl.ANY)
+    hbm = pl.BlockSpec(memory_space=pltpu.HBM)
     whole = pl.BlockSpec(memory_space=pltpu.VMEM)
     return pl.pallas_call(
         functools.partial(main_kernel, rows_all, full),
@@ -460,7 +487,7 @@
             vm((16, 8, 128), F32),
             vm((8, 8, 128), F32),
             dma((3,)),
-            dma((18,)), dma((18,)),
+            dma((21,)), dma((21,)),
             dma((17,)), dma((17,)),
             dma((5,)), dma((1,)),
             dma((8,)), dma((8,)),
@@ -471,7 +498,7 @@
             dma((8,)), dma((8,)),
             dma((8,)), dma((8,)),
         ],
-        compiler_params=pltpu.CompilerParams(collective_id=0, has_side_effects=True, vmem_limit_bytes=60 * 2**20),
+        compiler_params=pltpu.CompilerParams(collective_id=0, has_side_effects=True, vmem_limit_bytes=36 * 2**20),
     )(tokens, gate_weight, up_weight, route.reshape(8, rows), live.reshape(8, rows))
 
 
@@ -487,7 +514,7 @@
     return one(a[0], b[0]) + (one(a[0], b[1]) + one(a[1], b[0]))
 
 
-def outputs_kernel(hp_ref, hcol_ref, hl_ref, x_ref, ridge_ref, panel_ref, trailing_ref):
+def outputs_kernel(hp_ref, hcol_ref, hl_ref, x_ref, ridge_ref, panel_ref, trailing_ref, panel, trailing, sems):
     xh, z, core = (lax.axis_index(a) for a in ROW)
     xl, y = (lax.axis_index(a) for a in COL)
     ci, ri = xl * 4 + y, (xh * 4 + z) * 2 + core
@@ -503,23 +530,33 @@
         return gram / rows_all + jnp.where(jnp.logical_and(on_line, here), ridge, 0.0)
 
     right = pair(dot3_t(pair(with_ridge(cross(hcol, hp), ri == 0)), x))
+    copies = []
     for j in range(2):
+        here = pl.ds(j * n, n)
         left = hl_ref[j].reshape(rows_all, n)
         down = dot3_t(pair(with_ridge(cross(left, hp), ci * 2 + j == 0)), x)
-        panel_ref[pl.ds(j * n, n), :] = down
-        trailing_ref[pl.ds(j * n, n), :] = with_ridge(cross(left, hcol), ci * 2 + j == ri) - dot3_t(pair(down), right)
+        panel[here, :] = down
+        copies.append(pltpu.make_async_copy(panel.at[here], panel_ref.at[here], sems.at[j]))
+        copies[-1].start()
+        trailing[here, :] = with_ridge(cross(left, hcol), ci * 2 + j == ri) - dot3_t(pair(down), right)
+        copies.append(pltpu.make_async_copy(trailing.at[here], trailing_ref.at[here], sems.at[2 + j]))
+        copies[-1].start()
+    for copy in copies:
+        copy.wait()
 
 
 def outputs_of(hp, hcol, hl, x, ridge):
     n = x.shape[0]
+    hbm = pl.BlockSpec(memory_space=pl.ANY)
     whole = pl.BlockSpec(memory_space=pltpu.VMEM)
     return pl.pallas_call(
         outputs_kernel,
         name="outputs",
         out_shape=(jax.ShapeDtypeStruct((2 * n, n), F32), jax.ShapeDtypeStruct((2 * n, n), F32)),
         in_specs=[whole] * 5,
-        out_specs=(whole, whole),
-        compiler_params=pltpu.CompilerParams(vmem_limit_bytes=60 * 2**20),
+        out_specs=(hbm, hbm),
+        scratch_shapes=[pltpu.VMEM((2 * n, n), F32), pltpu.VMEM((2 * n, n), F32), pltpu.SemaphoreType.DMA((4,))],
+        compiler_params=pltpu.CompilerParams(vmem_limit_bytes=28 * 2**20),
     )(hp, hcol, hl, x, ridge)
 
 

time: 126 us -> 119 us (0.944)
  Pallas kernels: 124 us -> 112 us
  local copies, waits for them, and re-layouts: 0 us -> 4.56 us
    pallas_call x1, Pallas kernels: 113 us -> 104 us  [main_of(): pl.pallas_call(functools.partial(main_kernel, rows_all, full), name='hidd...]
    unnamed x0 -> x10, local copies, waits for them, and re-layouts: none -> 4.56 us
    pallas_call x1, Pallas kernels: 10.9 us -> 8.01 us  [outputs_of(): pl.pallas_call(outputs_kernel, name='outputs', out_shape=(jax.ShapeDtypeS...]
where the time goes in v4:
time: 119 us; the launch traced here: 117 us
  Pallas kernels  112 us (94%)
  local copies, waits for them, and re-layouts  4.56 us (4%)
    pallas_call x1, Pallas kernels, main_of(): pl.pallas_call(functools.partial(main_kernel, rows_all, full), name='hidd...  104 us
    pallas_call x1, Pallas kernels, outputs_of(): pl.pallas_call(outputs_kernel, name='outputs', out_shape=(jax.ShapeDtypeS...  8.01 us
    unnamed x10, local copies, waits for them, and re-layouts  4.56 us

profile of v4, /device:TPU:87, one launch (start us, length us, event | category | flops | bytes accessed | tf_op | source)
XLA Modules:
  0.0 117.4 jit_solution(5185682594385319199)
XLA Ops:
  0.6 0.0 copy-start
  0.6 1.1 copy-done
  1.8 0.0 copy-start.1
  1.8 1.1 copy-done.1
  2.9 0.0 copy-start.2
  2.9 0.9 copy-done.2
  3.8 0.0 copy-start.3
  3.8 0.7 copy-done.3
  4.5 0.0 copy-start.4
  4.5 0.7 copy-done.4
  5.2 104.0 %hidden_factor.1 = (bf16[8,128,512]{2,1,0:T(8,128)(2,1)S(1)}, bf16[8,128,512]{2,1,0:T(8,128)(2,1)S(1)}, bf16[2,8,128,512]{3,2,1,0:T(8,128)(2,1)S(1)}, f32[512,512]{1,0:T(8,128)S(1)}, f32[8,128]{1,0:T(8,128)S(1)}) custom-call(bf16[128,768]{1,0:T(8,128)(2,1)S(1)} %copy-done.2, bf16[768,512]{1,0:T(8,128)(2,1)S(1)} %copy-done, bf16[768,512]{1,0:T(8,128)(2,1)S(1)} %copy-done.1, ...), custom_call_target="tpu_custom_call" | custom-call | tf_op jit(solution)/shard_map/hidden_factor/pallas_call | solution.py:459
  109.2 8.0 %outputs.1 = (f32[1024,512]{1,0:T(8,128)}, f32[1024,512]{1,0:T(8,128)}) custom-call(bf16[8,128,512]{2,1,0:T(8,128)(2,1)S(1)} %get-tuple-element.7.hp_ref, bf16[8,128,512]{2,1,0:T(8,128)(2,1)S(1)} %get-tuple-element.8.hcol_ref, bf16[2,8,128,512]{3,2,1,0:T(8,128)(2,1)S(1)} %get-tuple-element.9.hl_ref, f32[512,512]{1,0:T(8,128)S(1)} %get-tuple-element.10.x_ref, ...), custom_call_target="tpu_custom_call" | custom-call | tf_op jit(solution)/shard_map/outputs/pallas_call | solution.py:552
Async XLA Ops:
  0.6 1.1 copy-start
  1.8 1.1 copy-start.1
  2.9 0.9 copy-start.2
  3.8 0.7 copy-start.3
  4.5 0.7 copy-start.4

commit v5 on v4

--- a/solution.py
+++ b/solution.py
@@ -112,9 +112,9 @@
 
 
 def main_kernel(
-    total_rows, full, tok_ref, gate_ref, up_ref, route_ref, live_ref,
+    total_rows, full, tok_ref, gate_ref, up_ref, route_in, live_in,
     hp_ref, hcol_ref, hl_ref, x_ref, ridge_ref,
-    tk, gw, uw, spots, tg, tu, rgx, rg1, rg2, ru1, ru2, rux, uout, hid, corner, tr, tc, own_sem,
+    tk, gw, uw, route_ref, live_ref, spots, tg, tu, rgx, rg1, rg2, ru1, ru2, rux, uout, hid, corner, tr, tc, own_sem,
     a_send, a_recv, r_send, r_recv, p1s, p1r, p2s, p2r, p3s, p3r, ts, tq, us, ur, hs, hr_sem, qs, qr, ls, lr,
 ):
     xh, z, core = (lax.axis_index(a) for a in ROW)
@@ -140,6 +140,12 @@
 
     own = pltpu.make_async_copy(tok_ref, tk.at[xh, z, core], own_sem.at[0])
     own.start()
+    lists = [
+        pltpu.make_async_copy(src, dst, own_sem.at[3 + i])
+        for i, (src, dst) in enumerate(((route_in, route_ref), (live_in, live_ref)))
+    ]
+    for copy in lists:
+        copy.start()
     gcopy = pltpu.make_async_copy(gate_ref, gw, own_sem.at[1])
     gcopy.start()
     ucopy = pltpu.make_async_copy(up_ref, uw, own_sem.at[2])
@@ -153,6 +159,8 @@
         pl.semaphore_signal(barrier, inc=1, device_id=mirror, device_id_type=MESH)
 
     rows = total_rows // 8
+    for copy in lists:
+        copy.wait()
     for t in range(8):
         spots[pl.ds(t * rows, rows), :] = turned(route_ref[t:t + 1, :]).astype(jnp.int32)
     own.wait()
@@ -307,6 +315,22 @@
     def _():
         hp_ref[ci, pl.ds(0, half)] = made[:half]
         give.start()
+        for hop in hops:
+            hop.start()
+
+    along = ((1, to_yn), (3, to_yp), (2, {"col_1": yf}))
+    across = remote(hid, hl_ref.at[core, ci], (qs, qr), 0, mirror)
+    stay = pltpu.make_async_copy(hid, hl_ref.at[core, ci], own_sem.at[0])
+    four, five, six = (hs, hr_sem), (qs, qr), (ls, lr)
+    cp = ol * 4 + y
+
+    @pl.when(away)
+    def _():
+        across.start()
+
+    @pl.when(jnp.logical_not(away))
+    def _():
+        stay.start()
 
     wide = made.astype(F32)
     squares = jnp.zeros((8, 128), F32)
@@ -322,39 +346,41 @@
     def _():
         arrive((p1s, p1r), 0, mine)
 
-    @pl.when(at_root)
+    @pl.when(jnp.logical_and(at_root, core == 1))
     def _():
         hops[0].start()
 
-    @pl.when(z == 0)
+    @pl.when(jnp.logical_and(z == 0, jnp.logical_not(holder)))
     def _():
         for hop in hops[1:]:
             hop.start()
 
     two, three = (p2s, p2r), (p3s, p3r)
-    along = ((1, to_yn), (3, to_yp), (2, {"col_1": yf}))
-    across = remote(hid, hl_ref.at[core, ci], (qs, qr), 0, mirror)
-    stay = pltpu.make_async_copy(hid, hl_ref.at[core, ci], own_sem.at[0])
-    four, five, six = (hs, hr_sem), (qs, qr), (ls, lr)
-    cp = ol * 4 + y
     pass_on(two, 4, mine, to_l)
     for d, where in along:
         pass_on(two, d, mine, where)
     pass_on(three, 0, mine, to_core)
+
+    def spread_block(h, zz, k):
+        return hl_ref.at[k, h * 4 + zz]
+
+    here = spread_block(xh, z, core)
+
+    @pl.when(away)
+    def _():
+        across.wait_recv()
+
+    @pl.when(jnp.logical_not(away))
+    def _():
+        stay.wait()
+
+    for slot, where in ((1, to_x), (2, to_zn), (3, to_zp), (4, to_zf)):
+        pass_on(five, slot, here, where)
     arrive(two, 4, by_half(cp, core))
     for d, where in along:
         pass_on(two, 4 + d, by_half(cp, core), where)
     pass_on(three, 4, by_half(cp, core), to_core)
     send(four, 4, hid, hcol_ref.at[ci], to_l)
-
-    @pl.when(away)
-    def _():
-        across.start()
-
-    @pl.when(jnp.logical_not(away))
-    def _():
-        stay.start()
-
     for s in row_steps:
         arrive((ts, tq), s[0] * 8 + s[1] * 2 + s[2], tr.at[row_from[s]])
     tc[ci] = jnp.sum(tr[...], axis=0)
@@ -367,11 +393,11 @@
         slot = s[0] * 4 + s[1]
         arrive(two, slot, by_half(col_from[s], core))
         pass_on(three, slot, by_half(col_from[s], core), to_core)
-
-    def spread_block(h, zz, k):
-        return hl_ref.at[k, h * 4 + zz]
-
-    here = spread_block(xh, z, core)
+    arrive(five, 1, spread_block(oh, z, core))
+    for slot, where in ((5, to_zn), (6, to_zp), (7, to_zf)):
+        pass_on(five, slot, spread_block(oh, z, core), where)
+    pass_on(six, 0, here, to_core)
+    pass_on(six, 1, spread_block(oh, z, core), to_core)
     arrive(three, 0, by_half(ci, oc))
     arrive(three, 4, by_half(cp, oc))
     for s in order:
@@ -394,27 +420,11 @@
             for d, where in along:
                 pass_on(four, 4 + d, hcol_ref.at[cp], where)
 
-            @pl.when(away)
-            def _():
-                across.wait_recv()
-
-            @pl.when(jnp.logical_not(away))
-            def _():
-                stay.wait()
-
-            for slot, where in ((1, to_x), (2, to_zn), (3, to_zp), (4, to_zf)):
-                pass_on(five, slot, here, where)
-            pass_on(six, 0, here, to_core)
-        elif k == 3:
-            arrive(five, 1, spread_block(oh, z, core))
-            for slot, where in ((5, to_zn), (6, to_zp), (7, to_zf)):
-                pass_on(five, slot, spread_block(oh, z, core), where)
-            pass_on(six, 1, spread_block(oh, z, core), to_core)
-        elif k == 4:
+        elif k == 2:
             for slot, zz in ((2, zp), (3, zn), (4, zf)):
                 arrive(five, slot, spread_block(xh, zz, core))
                 pass_on(six, slot, spread_block(xh, zz, core), to_core)
-        elif k == 6:
+        elif k == 5:
             for slot, zz in ((5, zp), (6, zn), (7, zf)):
                 arrive(five, slot, spread_block(oh, zz, core))
                 pass_on(six, slot, spread_block(oh, zz, core), to_core)
@@ -456,6 +466,7 @@
     dma = pltpu.SemaphoreType.DMA
     hbm = pl.BlockSpec(memory_space=pltpu.HBM)
     whole = pl.BlockSpec(memory_space=pltpu.VMEM)
+    operands = (tokens, gate_weight, up_weight, route.reshape(8, rows), live.reshape(8, rows))
     return pl.pallas_call(
         functools.partial(main_kernel, rows_all, full),
         name="hidden_factor",
@@ -466,12 +477,14 @@
             jax.ShapeDtypeStruct((PANEL, PANEL), F32),
             jax.ShapeDtypeStruct((8, 128), F32),
         ),
-        in_specs=[hbm, hbm, hbm, whole, whole],
+        in_specs=[hbm] * 5,
         out_specs=(whole,) * 5,
         scratch_shapes=[
             vm((2, 4, 2, m, width), BF16),
             vm(gate_weight.shape, BF16),
             vm(up_weight.shape, BF16),
+            vm((8, rows), jnp.int32),
+            vm((8, rows), jnp.int32),
             vm((rows_all, 128), jnp.int32),
             vm((2, 4, rows, own), F32),
             vm((2, 4, rows, own), F32),
@@ -486,7 +499,7 @@
             vm((PANEL, PANEL), F32),
             vm((16, 8, 128), F32),
             vm((8, 8, 128), F32),
-            dma((3,)),
+            dma((5,)),
             dma((21,)), dma((21,)),
             dma((17,)), dma((17,)),
             dma((5,)), dma((1,)),
@@ -498,8 +511,8 @@
             dma((8,)), dma((8,)),
             dma((8,)), dma((8,)),
         ],
-        compiler_params=pltpu.CompilerParams(collective_id=0, has_side_effects=True, vmem_limit_bytes=36 * 2**20),
-    )(tokens, gate_weight, up_weight, route.reshape(8, rows), live.reshape(8, rows))
+        compiler_params=pltpu.CompilerParams(collective_id=0, has_side_effects=True, vmem_limit_bytes=46000 * 2**10),
+    )(*(pltpu.with_memory_space_constraint(a, pltpu.HBM) for a in operands))
 
 
 def pair(a):

time: 119 us -> 111 us (0.933)
  local copies, waits for them, and re-layouts: 4.56 us -> 0 us
  Pallas kernels: 112 us -> 110 us
    unnamed x10 -> x0, local copies, waits for them, and re-layouts: 4.56 us -> none
    pallas_call x1, Pallas kernels: 104 us -> 102 us  [main_of(): pl.pallas_call(functools.partial(main_kernel, rows_all, full), name='hidd...]
where the time goes in v5:
time: 111 us
  Pallas kernels  110 us (99%)
    pallas_call x1, Pallas kernels, main_of(): pl.pallas_call(functools.partial(main_kernel, rows_all, full), name='hidd...  102 us
    pallas_call x1, Pallas kernels, outputs_of(): pl.pallas_call(outputs_kernel, name='outputs', out_shape=(jax.ShapeDtypeS...  7.99 us

profile of v5, /device:TPU:87, one launch (start us, length us, event | category | flops | bytes accessed | tf_op | source)
XLA Modules:
  0.0 110.6 jit_solution(15757171997197352606)
XLA Ops:
  0.6 101.8 %hidden_factor.1 = (bf16[8,128,512]{2,1,0:T(8,128)(2,1)S(1)}, bf16[8,128,512]{2,1,0:T(8,128)(2,1)S(1)}, bf16[2,8,128,512]{3,2,1,0:T(8,128)(2,1)S(1)}, f32[512,512]{1,0:T(8,128)S(1)}, f32[8,128]{1,0:T(8,128)S(1)}) custom-call(bf16[128,768]{1,0:T(8,128)(2,1)} %tok_ref.1, bf16[768,512]{1,0:T(8,128)(2,1)} %gate_ref.1, bf16[768,512]{1,0:T(8,128)(2,1)} %up_ref.1, ...), custom_call_target="tpu_custom_call" | custom-call | tf_op jit(solution)/shard_map/hidden_factor/pallas_call | solution.py:470
  102.4 8.0 %outputs.1 = (f32[1024,512]{1,0:T(8,128)}, f32[1024,512]{1,0:T(8,128)}) custom-call(bf16[8,128,512]{2,1,0:T(8,128)(2,1)S(1)} %get-tuple-element.7.hp_ref, bf16[8,128,512]{2,1,0:T(8,128)(2,1)S(1)} %get-tuple-element.8.hcol_ref, bf16[2,8,128,512]{3,2,1,0:T(8,128)(2,1)S(1)} %get-tuple-element.9.hl_ref, f32[512,512]{1,0:T(8,128)S(1)} %get-tuple-element.10.x_ref, ...), custom_call_target="tpu_custom_call" | custom-call | tf_op jit(solution)/shard_map/outputs/pallas_call | solution.py:565

commit v6 on v5

--- a/solution.py
+++ b/solution.py
@@ -42,34 +42,36 @@
     rows = list(rows)
     out = []
     for g in range(count):
-        column = [[spread(rows[i][:, 8 * g + c:8 * g + c + 1]) for c in range(8)] for i in range(g, count)]
-        e = [[spread(column[0][b][a:a + 1, :]) for b in range(a + 1)] for a in range(8)]
+        top = [spread(rows[g][:, 8 * g + c:8 * g + c + 1]) for c in range(8)]
+        e = [[spread(top[b][a:a + 1, :]) for b in range(a + 1)] for a in range(8)]
         inside = (lane >= 8 * g) & (lane < 8 * g + 8)
-        rows[g] = jnp.where(inside, (lane == sub + 8 * g).astype(F32), rows[g])
+        group = jnp.where(inside, (lane == sub + 8 * g).astype(F32), rows[g])
+        own = [spread(group[c:c + 1, :]) for c in range(8)]
+        inverse = [None] * 8
+        m = [[None] * 8 for _ in range(8)]
+        for c in range(8):
+            if c % 2 == 0:
+                inverse[c] = 1.0 / e[c][c]
+                inverse[c + 1] = e[c][c] / (e[c][c] * e[c + 1][c + 1] - e[c + 1][c] * e[c + 1][c])
+            for a in range(c + 1, 8):
+                m[a][c] = e[a][c] * inverse[c]
+                for b in range(c + 1, a + 1):
+                    e[a][b] = e[a][b] - m[a][c] * e[b][c]
+                own[a] = own[a] - m[a][c] * own[c]
+        back = [own[c] * inverse[c] for c in range(8)]
+        for b in range(7, 0, -1):
+            for c in range(b):
+                back[c] = back[c] - m[b][c] * back[b]
         for i in range(g + 1, count):
-            rows[i] = jnp.where(inside, 0.0, rows[i])
-        pivots = e[0][0]
-        for c in range(8):
-            if c:
-                pivots = jnp.where(sub == c, e[c][c], pivots)
-            if c % 2 == 0:
-                inverse = 1.0 / e[c][c]
-                later = e[c][c] / (e[c][c] * e[c + 1][c + 1] - e[c + 1][c] * e[c + 1][c])
-            else:
-                inverse = later
-            for a in range(c + 1, 8):
-                factor = e[a][c] * inverse
-                for b in range(c + 1, a + 1):
-                    e[a][b] = e[a][b] - factor * e[b][c]
-            pivot_row = spread(rows[g][c:c + 1, :])
-            for i in range(g, count):
-                factor = column[i - g][c] * inverse
-                if i == g:
-                    factor = jnp.where(sub > c, factor, 0.0)
-                for b in range(c + 1, 8):
-                    column[i - g][b] = column[i - g][b] - factor * e[b][c]
-                rows[i] = rows[i] - factor * pivot_row
-        out.append(jnp.where(lane <= sub + 8 * g, rows[g] * lax.rsqrt(pivots), 0.0))
+            terms = [spread(rows[i][:, 8 * g + c:8 * g + c + 1]) * back[c] for c in range(8)]
+            while len(terms) > 1:
+                terms = [terms[k] + terms[k + 1] for k in range(0, len(terms), 2)]
+            rows[i] = jnp.where(inside, 0.0, rows[i]) - terms[0]
+        pivots, done = e[0][0], own[0]
+        for c in range(1, 8):
+            pivots = jnp.where(sub == c, e[c][c], pivots)
+            done = jnp.where(sub == c, own[c], done)
+        out.append(jnp.where(lane <= sub + 8 * g, done * lax.rsqrt(pivots), 0.0))
         if g == count // 2 - 1:
             halfway()
     return out
@@ -114,8 +116,8 @@
 def main_kernel(
     total_rows, full, tok_ref, gate_ref, up_ref, route_in, live_in,
     hp_ref, hcol_ref, hl_ref, x_ref, ridge_ref,
-    tk, gw, uw, route_ref, live_ref, spots, tg, tu, rgx, rg1, rg2, ru1, ru2, rux, uout, hid, corner, tr, tc, own_sem,
-    a_send, a_recv, r_send, r_recv, p1s, p1r, p2s, p2r, p3s, p3r, ts, tq, us, ur, hs, hr_sem, qs, qr, ls, lr,
+    tk, gw, uw, route_ref, live_ref, spots, tg, tu, rgx, rg1, rg2, ru1, ru2, rux, uout, hid, corner, tr, tz, ty, own_sem,
+    a_send, a_recv, r_send, r_recv, p1s, p1r, p2s, p2r, p3s, p3r, ts, tq, hs, hr_sem, qs, qr, ls, lr,
 ):
     xh, z, core = (lax.axis_index(a) for a in ROW)
     xl, y = (lax.axis_index(a) for a in COL)
@@ -131,12 +133,9 @@
     away = jnp.logical_or(xh != xl, z != y)
     m = tok_ref.shape[0]
     cut = m * 5 // 8
-    col_steps = [(a, b) for a in range(2) for b in range(4) if a + b]
-    row_steps = [(a, b, c) for a in range(2) for b in range(4) for c in range(2) if a + b + c]
-    col_peer = {s: {"col_0": (xl + s[0]) % 2, "col_1": (y + s[1]) % 4} for s in col_steps}
-    col_from = {s: (xl + s[0]) % 2 * 4 + (y + 4 - s[1]) % 4 for s in col_steps}
-    row_peer = {s: {"row_0": (xh + s[0]) % 2, "row_1": (z + s[1]) % 4, "row_2": (core + s[2]) % 2} for s in row_steps}
-    row_from = {s: ((xh + s[0]) % 2 * 4 + (z + 4 - s[1]) % 4) * 2 + (core + s[2]) % 2 for s in row_steps}
+    to_yf = {"col_1": yf}
+    peers = [to_x, to_core, to_zn, to_zp, to_zf, to_l, to_yn, to_yp, to_yf]
+    col_from = {(a, b): (xl + a) % 2 * 4 + (y + 4 - b) % 4 for a in range(2) for b in range(4)}
 
     own = pltpu.make_async_copy(tok_ref, tk.at[xh, z, core], own_sem.at[0])
     own.start()
@@ -151,7 +150,7 @@
     ucopy = pltpu.make_async_copy(up_ref, uw, own_sem.at[2])
     ucopy.start()
     barrier = pltpu.get_barrier_semaphore()
-    for peer in list(col_peer.values()) + list(row_peer.values()):
+    for peer in peers:
         pl.semaphore_signal(barrier, inc=1, device_id=peer, device_id_type=MESH)
 
     @pl.when(away)
@@ -164,15 +163,14 @@
     for t in range(8):
         spots[pl.ds(t * rows, rows), :] = turned(route_ref[t:t + 1, :]).astype(jnp.int32)
     own.wait()
-    peers = len(col_steps) + len(row_steps)
 
     @pl.when(away)
     def _():
-        pl.semaphore_wait(barrier, peers + 1)
+        pl.semaphore_wait(barrier, len(peers) + 1)
 
     @pl.when(jnp.logical_not(away))
     def _():
-        pl.semaphore_wait(barrier, peers)
+        pl.semaphore_wait(barrier, len(peers))
 
     started = []
 
@@ -318,7 +316,7 @@
         for hop in hops:
             hop.start()
 
-    along = ((1, to_yn), (3, to_yp), (2, {"col_1": yf}))
+    along = ((1, to_yn), (3, to_yp), (2, to_yf))
     across = remote(hid, hl_ref.at[core, ci], (qs, qr), 0, mirror)
     stay = pltpu.make_async_copy(hid, hl_ref.at[core, ci], own_sem.at[0])
     four, five, six = (hs, hr_sem), (qs, qr), (ls, lr)
@@ -338,13 +336,17 @@
         for j in range(0, hid.shape[1], 128):
             piece = wide[i:i + 8, j:j + 128]
             squares = squares + piece * piece
-    tr[ri] = squares
-    for s in row_steps:
-        send((ts, tq), s[0] * 8 + s[1] * 2 + s[2], tr.at[ri], tr.at[ri], row_peer[s])
+    seven = (ts, tq)
+    tr[0] = squares
+    send(seven, 0, tr.at[0], tr.at[1], to_core)
 
     @pl.when(jnp.logical_not(holder))
     def _():
         arrive((p1s, p1r), 0, mine)
+
+    arrive(seven, 0, tr.at[1])
+    tr[2] = tr[0] + tr[1]
+    send(seven, 1, tr.at[2], tr.at[3], to_x)
 
     @pl.when(jnp.logical_and(at_root, core == 1))
     def _():
@@ -376,16 +378,19 @@
 
     for slot, where in ((1, to_x), (2, to_zn), (3, to_zp), (4, to_zf)):
         pass_on(five, slot, here, where)
+    arrive(seven, 1, tr.at[3])
+    tz[z] = tr[2] + tr[3]
+    for d, where in ((1, to_zn), (3, to_zp), (2, to_zf)):
+        pass_on(seven, 1 + d, tz.at[z], where)
     arrive(two, 4, by_half(cp, core))
     for d, where in along:
         pass_on(two, 4 + d, by_half(cp, core), where)
     pass_on(three, 4, by_half(cp, core), to_core)
     send(four, 4, hid, hcol_ref.at[ci], to_l)
-    for s in row_steps:
-        arrive((ts, tq), s[0] * 8 + s[1] * 2 + s[2], tr.at[row_from[s]])
-    tc[ci] = jnp.sum(tr[...], axis=0)
-    for s in col_steps:
-        send((us, ur), s[0] * 4 + s[1], tc.at[ci], tc.at[ci], col_peer[s])
+    for d, zz in ((1, zp), (3, zn), (2, zf)):
+        arrive(seven, 1 + d, tz.at[zz])
+    tr[4] = jnp.sum(tz[...], axis=0)
+    send(seven, 5, tr.at[4], tr.at[5], to_l)
     for d, where in along:
         send(four, d, hid, hcol_ref.at[ci], where)
     order = [(0, 1), (0, 3), (0, 2), (1, 1), (1, 3), (1, 2)]
@@ -393,6 +398,11 @@
         slot = s[0] * 4 + s[1]
         arrive(two, slot, by_half(col_from[s], core))
         pass_on(three, slot, by_half(col_from[s], core), to_core)
+        if s == (0, 2):
+            arrive(seven, 5, tr.at[5])
+            ty[y] = tr[4] + tr[5]
+            for d, where in along:
+                pass_on(seven, 5 + d, ty.at[y], where)
     arrive(five, 1, spread_block(oh, z, core))
     for slot, where in ((5, to_zn), (6, to_zp), (7, to_zf)):
         pass_on(five, slot, spread_block(oh, z, core), where)
@@ -406,9 +416,9 @@
     hp = hp_ref[...].reshape(total_rows, panel)
     on_line = lax.broadcasted_iota(jnp.int32, (panel, panel), 0) == lax.broadcasted_iota(jnp.int32, (panel, panel), 1)
     gram = cross(hp, hp) / total_rows
-    for s in col_steps:
-        arrive((us, ur), s[0] * 4 + s[1], tc.at[col_from[s]])
-    total = jnp.sum(jnp.sum(tc[...], axis=0), axis=(0, 1), keepdims=True)
+    for d, yy in ((1, yp), (3, yn), (2, yf)):
+        arrive(seven, 5 + d, ty.at[yy])
+    total = jnp.sum(jnp.sum(ty[...], axis=0), axis=(0, 1), keepdims=True)
     ridge = damping * total / (total_rows * full)
     ridge_ref[...] = jnp.broadcast_to(ridge, (8, 128))
     scale = 1.0 / ridge
@@ -497,16 +507,16 @@
             vm((rows, own), F32),
             vm((rows, own), BF16),
             vm((PANEL, PANEL), F32),
-            vm((16, 8, 128), F32),
-            vm((8, 8, 128), F32),
+            vm((6, 8, 128), F32),
+            vm((4, 8, 128), F32),
+            vm((4, 8, 128), F32),
             dma((5,)),
             dma((21,)), dma((21,)),
             dma((17,)), dma((17,)),
             dma((5,)), dma((1,)),
             dma((8,)), dma((8,)),
             dma((8,)), dma((8,)),
-            dma((16,)), dma((16,)),
-            dma((8,)), dma((8,)),
+            dma((9,)), dma((9,)),
             dma((8,)), dma((8,)),
             dma((8,)), dma((8,)),
             dma((8,)), dma((8,)),

time: 111 us -> 113 us (1.018)
  the two profiles are of different devices: /device:TPU:87 before, /device:TPU:7 now
where the time goes in v6:
time: 113 us
  Pallas kernels  112 us (99%)
    pallas_call x1, Pallas kernels, main_of(): pl.pallas_call(functools.partial(main_kernel, rows_all, full), name='hidd...  104 us
    pallas_call x1, Pallas kernels, outputs_of(): pl.pallas_call(outputs_kernel, name='outputs', out_shape=(jax.ShapeDtypeS...  7.99 us

profile of v6, /device:TPU:7, one launch (start us, length us, event | category | flops | bytes accessed | tf_op | source)
XLA Modules:
  0.0 112.8 jit_solution(3390909201748426419)
XLA Ops:
  0.6 104.0 %hidden_factor.1 = (bf16[8,128,512]{2,1,0:T(8,128)(2,1)S(1)}, bf16[8,128,512]{2,1,0:T(8,128)(2,1)S(1)}, bf16[2,8,128,512]{3,2,1,0:T(8,128)(2,1)S(1)}, f32[512,512]{1,0:T(8,128)S(1)}, f32[8,128]{1,0:T(8,128)S(1)}) custom-call(bf16[128,768]{1,0:T(8,128)(2,1)} %tok_ref.1, bf16[768,512]{1,0:T(8,128)(2,1)} %gate_ref.1, bf16[768,512]{1,0:T(8,128)(2,1)} %up_ref.1, ...), custom_call_target="tpu_custom_call" | custom-call | tf_op jit(solution)/shard_map/hidden_factor/pallas_call | solution.py:480
  104.7 8.0 %outputs.1 = (f32[1024,512]{1,0:T(8,128)}, f32[1024,512]{1,0:T(8,128)}) custom-call(bf16[8,128,512]{2,1,0:T(8,128)(2,1)S(1)} %get-tuple-element.7.hp_ref, bf16[8,128,512]{2,1,0:T(8,128)(2,1)S(1)} %get-tuple-element.8.hcol_ref, bf16[2,8,128,512]{3,2,1,0:T(8,128)(2,1)S(1)} %get-tuple-element.9.hl_ref, f32[512,512]{1,0:T(8,128)S(1)} %get-tuple-element.10.x_ref, ...), custom_call_target="tpu_custom_call" | custom-call | tf_op jit(solution)/shard_map/outputs/pallas_call | solution.py:575

commit v7 on v6

--- a/solution.py
+++ b/solution.py
@@ -339,14 +339,13 @@
     seven = (ts, tq)
     tr[0] = squares
     send(seven, 0, tr.at[0], tr.at[1], to_core)
-
-    @pl.when(jnp.logical_not(holder))
-    def _():
-        arrive((p1s, p1r), 0, mine)
-
     arrive(seven, 0, tr.at[1])
     tr[2] = tr[0] + tr[1]
     send(seven, 1, tr.at[2], tr.at[3], to_x)
+
+    @pl.when(jnp.logical_not(holder))
+    def _():
+        arrive((p1s, p1r), 0, mine)
 
     @pl.when(jnp.logical_and(at_root, core == 1))
     def _():
@@ -366,33 +365,31 @@
     def spread_block(h, zz, k):
         return hl_ref.at[k, h * 4 + zz]
 
-    here = spread_block(xh, z, core)
-
-    @pl.when(away)
-    def _():
-        across.wait_recv()
-
-    @pl.when(jnp.logical_not(away))
-    def _():
-        stay.wait()
-
-    for slot, where in ((1, to_x), (2, to_zn), (3, to_zp), (4, to_zf)):
-        pass_on(five, slot, here, where)
     arrive(seven, 1, tr.at[3])
     tz[z] = tr[2] + tr[3]
     for d, where in ((1, to_zn), (3, to_zp), (2, to_zf)):
         pass_on(seven, 1 + d, tz.at[z], where)
+    here = spread_block(xh, z, core)
+
+    @pl.when(away)
+    def _():
+        across.wait_recv()
+
+    @pl.when(jnp.logical_not(away))
+    def _():
+        stay.wait()
+
+    for slot, where in ((1, to_x), (2, to_zn), (3, to_zp), (4, to_zf)):
+        pass_on(five, slot, here, where)
     arrive(two, 4, by_half(cp, core))
     for d, where in along:
         pass_on(two, 4 + d, by_half(cp, core), where)
     pass_on(three, 4, by_half(cp, core), to_core)
-    send(four, 4, hid, hcol_ref.at[ci], to_l)
     for d, zz in ((1, zp), (3, zn), (2, zf)):
         arrive(seven, 1 + d, tz.at[zz])
     tr[4] = jnp.sum(tz[...], axis=0)
     send(seven, 5, tr.at[4], tr.at[5], to_l)
-    for d, where in along:
-        send(four, d, hid, hcol_ref.at[ci], where)
+    send(four, 4, hid, hcol_ref.at[ci], to_l)
     order = [(0, 1), (0, 3), (0, 2), (1, 1), (1, 3), (1, 2)]
     for s in order:
         slot = s[0] * 4 + s[1]
@@ -403,6 +400,8 @@
             ty[y] = tr[4] + tr[5]
             for d, where in along:
                 pass_on(seven, 5 + d, ty.at[y], where)
+            for d, where in along:
+                send(four, d, hid, hcol_ref.at[ci], where)
     arrive(five, 1, spread_block(oh, z, core))
     for slot, where in ((5, to_zn), (6, to_zp), (7, to_zf)):
         pass_on(five, slot, spread_block(oh, z, core), where)

time: 113 us -> 107 us (0.947)
  the two profiles are of different devices: /device:TPU:7 before, /device:TPU:87 now
where the time goes in v7:
time: 107 us; the launch traced here: 105 us
  Pallas kernels  104 us (97%)
    pallas_call x1, Pallas kernels, main_of(): pl.pallas_call(functools.partial(main_kernel, rows_all, full), name='hidd...  96.1 us
    pallas_call x1, Pallas kernels, outputs_of(): pl.pallas_call(outputs_kernel, name='outputs', out_shape=(jax.ShapeDtypeS...  7.99 us

profile of v7, /device:TPU:87, one launch (start us, length us, event | category | flops | bytes accessed | tf_op | source)
XLA Modules:
  0.0 105.0 jit_solution(2247751869749295309)
XLA Ops:
  0.6 96.1 %hidden_factor.1 = (bf16[8,128,512]{2,1,0:T(8,128)(2,1)S(1)}, bf16[8,128,512]{2,1,0:T(8,128)(2,1)S(1)}, bf16[2,8,128,512]{3,2,1,0:T(8,128)(2,1)S(1)}, f32[512,512]{1,0:T(8,128)S(1)}, f32[8,128]{1,0:T(8,128)S(1)}) custom-call(bf16[128,768]{1,0:T(8,128)(2,1)} %tok_ref.1, bf16[768,512]{1,0:T(8,128)(2,1)} %gate_ref.1, bf16[768,512]{1,0:T(8,128)(2,1)} %up_ref.1, ...), custom_call_target="tpu_custom_call" | custom-call | tf_op jit(solution)/shard_map/hidden_factor/pallas_call | solution.py:479
  96.8 8.0 %outputs.1 = (f32[1024,512]{1,0:T(8,128)}, f32[1024,512]{1,0:T(8,128)}) custom-call(bf16[8,128,512]{2,1,0:T(8,128)(2,1)S(1)} %get-tuple-element.7.hp_ref, bf16[8,128,512]{2,1,0:T(8,128)(2,1)S(1)} %get-tuple-element.8.hcol_ref, bf16[2,8,128,512]{3,2,1,0:T(8,128)(2,1)S(1)} %get-tuple-element.9.hl_ref, f32[512,512]{1,0:T(8,128)S(1)} %get-tuple-element.10.x_ref, ...), custom_call_target="tpu_custom_call" | custom-call | tf_op jit(solution)/shard_map/outputs/pallas_call | solution.py:574

commit v8 on v7

--- a/solution.py
+++ b/solution.py
@@ -402,11 +402,6 @@
                 pass_on(seven, 5 + d, ty.at[y], where)
             for d, where in along:
                 send(four, d, hid, hcol_ref.at[ci], where)
-    arrive(five, 1, spread_block(oh, z, core))
-    for slot, where in ((5, to_zn), (6, to_zp), (7, to_zf)):
-        pass_on(five, slot, spread_block(oh, z, core), where)
-    pass_on(six, 0, here, to_core)
-    pass_on(six, 1, spread_block(oh, z, core), to_core)
     arrive(three, 0, by_half(ci, oc))
     arrive(three, 4, by_half(cp, oc))
     for s in order:
@@ -425,6 +420,11 @@
 
     def between(k):
         if k == 0:
+            arrive(five, 1, spread_block(oh, z, core))
+            for slot, where in ((5, to_zn), (6, to_zp), (7, to_zf)):
+                pass_on(five, slot, spread_block(oh, z, core), where)
+            pass_on(six, 0, here, to_core)
+            pass_on(six, 1, spread_block(oh, z, core), to_core)
             arrive(four, 4, hcol_ref.at[cp])
             for d, where in along:
                 pass_on(four, 4 + d, hcol_ref.at[cp], where)

time: 107 us -> 107 us (level)
  no operation moved by 1% of the time
where the time goes in v8:
time: 107 us; the launch traced here: 105 us
  Pallas kernels  104 us (97%)
    pallas_call x1, Pallas kernels, main_of(): pl.pallas_call(functools.partial(main_kernel, rows_all, full), name='hidd...  96.2 us
    pallas_call x1, Pallas kernels, outputs_of(): pl.pallas_call(outputs_kernel, name='outputs', out_shape=(jax.ShapeDtypeS...  7.99 us

profile of v8, /device:TPU:87, one launch (start us, length us, event | category | flops | bytes accessed | tf_op | source)
XLA Modules:
  0.0 105.0 jit_solution(16756145546607602275)
XLA Ops:
  0.6 96.2 %hidden_factor.1 = (bf16[8,128,512]{2,1,0:T(8,128)(2,1)S(1)}, bf16[8,128,512]{2,1,0:T(8,128)(2,1)S(1)}, bf16[2,8,128,512]{3,2,1,0:T(8,128)(2,1)S(1)}, f32[512,512]{1,0:T(8,128)S(1)}, f32[8,128]{1,0:T(8,128)S(1)}) custom-call(bf16[128,768]{1,0:T(8,128)(2,1)} %tok_ref.1, bf16[768,512]{1,0:T(8,128)(2,1)} %gate_ref.1, bf16[768,512]{1,0:T(8,128)(2,1)} %up_ref.1, ...), custom_call_target="tpu_custom_call" | custom-call | tf_op jit(solution)/shard_map/hidden_factor/pallas_call | solution.py:479
  96.8 8.0 %outputs.1 = (f32[1024,512]{1,0:T(8,128)}, f32[1024,512]{1,0:T(8,128)}) custom-call(bf16[8,128,512]{2,1,0:T(8,128)(2,1)S(1)} %get-tuple-element.7.hp_ref, bf16[8,128,512]{2,1,0:T(8,128)(2,1)S(1)} %get-tuple-element.8.hcol_ref, bf16[2,8,128,512]{3,2,1,0:T(8,128)(2,1)S(1)} %get-tuple-element.9.hl_ref, f32[512,512]{1,0:T(8,128)S(1)} %get-tuple-element.10.x_ref, ...), custom_call_target="tpu_custom_call" | custom-call | tf_op jit(solution)/shard_map/outputs/pallas_call | solution.py:574

commit v9 on v7

--- a/solution.py
+++ b/solution.py
@@ -227,7 +227,7 @@
     pool = 16 * m
     width = tk.shape[-1]
 
-    def tile(b):
+    def tile(b, slot):
         spot = jnp.concatenate(
             [spots[pl.ds(pl.multiple_of((e * 4 + b) * rows, rows), rows), :] for e in range(2)], axis=0
         )
@@ -235,24 +235,22 @@
         hot = (spot == lax.broadcasted_iota(jnp.int32, (2 * rows, pool), 1)).astype(F32).astype(BF16)
         chosen = jnp.dot(hot, tk[...].reshape(pool, width), preferred_element_type=F32).astype(BF16)
         g = jnp.dot(chosen, gw[...], preferred_element_type=F32)
+        for e in range(2):
+            tg[e, b] = g[e * rows:(e + 1) * rows]
+        send(R, slot, tg.at[ol, b], rgx.at[slot], to_l)
         u = jnp.dot(chosen, uw[...], preferred_element_type=F32)
         for e in range(2):
-            tg[e, b] = g[e * rows:(e + 1) * rows]
             tu[e, b] = u[e * rows:(e + 1) * rows]
 
     top, bottom = pl.ds(0, hr), pl.ds(hr, hr)
-    tile(yf)
-    send(R, 0, tg.at[ol, yf], rgx.at[0], to_l)
+    tile(yf, 0)
     send(R, 4, tu.at[0, yf], ru1.at[0], to_yn)
     send(R, 5, tu.at[1, yf], ru1.at[1], to_yp)
-    tile(yn)
-    send(R, 1, tg.at[ol, yn], rgx.at[1], to_l)
+    tile(yn, 1)
     send(R, 6, tu.at[1, yn], ru2.at[0, 1], to_yn)
-    tile(yp)
-    send(R, 2, tg.at[ol, yp], rgx.at[2], to_l)
+    tile(yp, 2)
     send(R, 7, tu.at[0, yp], ru2.at[1, 0], to_yp)
-    tile(y)
-    send(R, 3, tg.at[ol, y], rgx.at[3], to_l)
+    tile(y, 3)
     arrive(R, 4, ru1.at[0])
     tu[0, yn] = tu[0, yn] + ru1[0]
     send(R, 8, tu.at[0, yn], ru2.at[0, 0], to_yn)

time: 107 us -> 107 us (level)
  no operation moved by 1% of the time
where the time goes in v9:
time: 107 us; the launch traced here: 105 us
  Pallas kernels  104 us (97%)
    pallas_call x1, Pallas kernels, main_of(): pl.pallas_call(functools.partial(main_kernel, rows_all, full), name='hidd...  95.7 us
    pallas_call x1, Pallas kernels, outputs_of(): pl.pallas_call(outputs_kernel, name='outputs', out_shape=(jax.ShapeDtypeS...  7.99 us

profile of v9, /device:TPU:87, one launch (start us, length us, event | category | flops | bytes accessed | tf_op | source)
XLA Modules:
  0.0 104.5 jit_solution(921681629445632539)
XLA Ops:
  0.6 95.7 %hidden_factor.1 = (bf16[8,128,512]{2,1,0:T(8,128)(2,1)S(1)}, bf16[8,128,512]{2,1,0:T(8,128)(2,1)S(1)}, bf16[2,8,128,512]{3,2,1,0:T(8,128)(2,1)S(1)}, f32[512,512]{1,0:T(8,128)S(1)}, f32[8,128]{1,0:T(8,128)S(1)}) custom-call(bf16[128,768]{1,0:T(8,128)(2,1)} %tok_ref.1, bf16[768,512]{1,0:T(8,128)(2,1)} %gate_ref.1, bf16[768,512]{1,0:T(8,128)(2,1)} %up_ref.1, ...), custom_call_target="tpu_custom_call" | custom-call | tf_op jit(solution)/shard_map/hidden_factor/pallas_call | solution.py:477
  96.4 8.0 %outputs.1 = (f32[1024,512]{1,0:T(8,128)}, f32[1024,512]{1,0:T(8,128)}) custom-call(bf16[8,128,512]{2,1,0:T(8,128)(2,1)S(1)} %get-tuple-element.7.hp_ref, bf16[8,128,512]{2,1,0:T(8,128)(2,1)S(1)} %get-tuple-element.8.hcol_ref, bf16[2,8,128,512]{3,2,1,0:T(8,128)(2,1)S(1)} %get-tuple-element.9.hl_ref, f32[512,512]{1,0:T(8,128)S(1)} %get-tuple-element.10.x_ref, ...), custom_call_target="tpu_custom_call" | custom-call | tf_op jit(solution)/shard_map/outputs/pallas_call | solution.py:572
